TPU v7x, 512 devices: a whole 4x4x16 slice. The times are simulated.
512 devices in a mesh: space: 128 (over z, x, core), chan: 4 (over y).
Axes of the slice: x: 4, y: 4, z: 16, core: 2. Of those that a mesh axis runs over, the one named last changes fastest.
Arguments:
- features: bfloat16 [1024, 64, 512], P('space', 'chan'), may hold values from -6 to 6
- weight: bfloat16 [27, 64, 64], P(None, 'chan'), may hold values from -0.15625 to 0.15625
- cotangent: bfloat16 [1024, 64, 512], P('space', 'chan'), may hold values from -6 to 6
- neighbours: int32 [1024, 27], P('space'), may hold values from -1 to 1023, as said below
Outputs:
- output: bfloat16 [1024, 64, 512], P('space', 'chan')
- grad_input: bfloat16 [1024, 64, 512], P('space', 'chan')
- grad_weight: float32 [27, 64, 64], P(None, 'chan')
Inputs may be any that keep to these rules, and one draw needn't show every extreme that they name: `neighbours`: row r lists, for the displacement (i, j, k) in the finite set (-1, 0, 1)^3 at entry 9 (i + 1) + 3 (j + 1) + (k + 1), the slot of the brick at that displacement in bricks, or -1 where the scene has none. Slot s belongs to device s // 8 of space, and a neighbour at first displacement i belongs to the device of index one's own + i. The relation is symmetric: if row r names s at entry m, row s names r at entry 26 - m. A device's occupied bricks fill its first slots, and the last device of space has all 8 slots occupied; an empty slot's row is all -1, no row names an empty slot, and an occupied brick's entry 13 is its own slot.
All inputs are finite; a program needn't handle non-finite values.
Results may differ from a plain program's by a relative error of at most 0.001.
Values may be sent and summed in bfloat16 or wider, within the bound.
A program may use at most 128 MiB of HBM per device.

v0:
```python
import jax
import jax.numpy as jnp
import numpy as np
from jax import lax
from jax.sharding import PartitionSpec as P

flat_width = 896
source_width = 1152


def shifted(shard, axis, by):
    length = lax.axis_size(axis)
    pairs = [(i, i + by) for i in range(length) if 0 <= i + by < length]
    return lax.ppermute(shard, axis, pairs)


def axis_pairs(step):
    if step == 0:
        return [(0, 7)]
    if step == 1:
        return [(place + 1, place) for place in range(8)]
    return [(9, 0)]


def piece_tables():
    lists = []
    positions = []
    for step_x in range(3):
        for step_y in range(3):
            for step_z in range(3):
                source_ids = []
                for grid_x, vox_u in axis_pairs(step_x):
                    for grid_y, vox_v in axis_pairs(step_y):
                        for grid_z, vox_w in axis_pairs(step_z):
                            if step_x == 1:
                                source_ids.append(64 * vox_u + 8 * vox_v + vox_w)
                            else:
                                source_ids.append(8 * vox_v + vox_w)
                            positions.append(100 * grid_x + 10 * grid_y + grid_z)
                lists.append(np.array(source_ids, dtype=np.int32))
    order = np.argsort(np.array(positions, dtype=np.int64)).astype(np.int32)
    return (lists, order)


def grid_tables():
    into_grid = np.zeros((flat_width,), dtype=np.int32)
    valid = np.zeros((flat_width,), dtype=np.float32)
    back_ids = np.zeros((512,), dtype=np.int32)
    for vox_u in range(8):
        for vox_v in range(8):
            for vox_w in range(8):
                place = 100 * vox_u + 10 * vox_v + vox_w
                into_grid[place] = 64 * vox_u + 8 * vox_v + vox_w
                valid[place] = 1.0
                back_ids[64 * vox_u + 8 * vox_v + vox_w] = place
    return (into_grid, valid, back_ids)


def split_planes(bricks):
    return (bricks[..., 0:64], bricks[..., 448:512])


def neighbour_planes(bricks):
    previous = shifted(bricks, "space", 1)
    following = shifted(bricks, "space", -1)
    before_plane = split_planes(previous)[1]
    after_plane = split_planes(following)[0]
    return (before_plane, after_plane)


def spread(own_part):
    entire = lax.all_gather(own_part, "chan", axis=2, tiled=True)
    before_plane, after_plane = neighbour_planes(entire)
    return (entire, before_plane, after_plane)


def assemble(entire, before_plane, after_plane, table, own_start):
    brick_count, depth = (entire.shape[0], entire.shape[1])
    lists, order = piece_tables()
    sources = (
        jnp.concatenate([before_plane, jnp.zeros((1, depth, 64), entire.dtype)], axis=0),
        jnp.concatenate([entire, jnp.zeros((1, depth, 512), entire.dtype)], axis=0),
        jnp.concatenate([after_plane, jnp.zeros((1, depth, 64), entire.dtype)], axis=0),
    )
    pieces = []
    for step_x in range(3):
        block_start = own_start + (step_x - 1) * brick_count
        for step_y in range(3):
            for step_z in range(3):
                index_k = 9 * step_x + 3 * step_y + step_z
                listed = table[:, index_k]
                local_ids = jnp.where(listed < 0, brick_count, listed - block_start)
                picked = jnp.take(sources[step_x], local_ids, axis=0)
                pieces.append(jnp.take(picked, jnp.asarray(lists[index_k]), axis=2))
    joined = jnp.concatenate(pieces, axis=2)
    flat = jnp.take(joined, jnp.asarray(order), axis=2)
    return jnp.pad(flat, ((0, 0), (0, 0), (0, source_width - 1000)))


def to_padded_grid(bricks):
    into_grid, valid, back_ids = grid_tables()
    taken = jnp.take(bricks, jnp.asarray(into_grid), axis=2)
    return taken * jnp.asarray(valid).astype(bricks.dtype)


def from_padded_grid(flat):
    into_grid, valid, back_ids = grid_tables()
    return jnp.take(flat, jnp.asarray(back_ids), axis=2)


def body(features, weight, cotangent, neighbours):
    brick_count, narrow = (features.shape[0], features.shape[1])
    own_start = lax.axis_index("space") * brick_count
    feat_views = tuple((view[0] for view in spread(features[None])))
    grad_views = tuple((view[0] for view in spread(cotangent[None])))
    padded = assemble(feat_views[0], feat_views[1], feat_views[2], neighbours, own_start)
    grad_flat = to_padded_grid(cotangent)
    running = jnp.zeros((brick_count, narrow, flat_width), jnp.float32)
    kernel_terms = []
    for step_x in range(3):
        for step_y in range(3):
            for step_z in range(3):
                index_k = 9 * step_x + 3 * step_y + step_z
                offset = 100 * step_x + 10 * step_y + step_z
                window = padded[:, :, offset : offset + flat_width]
                running = running + jnp.einsum(
                    "oc,rcn->ron", weight[index_k], window, preferred_element_type=jnp.float32
                )
                kernel_terms.append(
                    jnp.einsum("ron,rcn->oc", grad_flat, window, preferred_element_type=jnp.float32)
                )
    output = from_padded_grid(running).astype(jnp.bfloat16)
    voxel_total = brick_count * lax.axis_size("space") * 512
    summed = lax.psum(jnp.stack(kernel_terms), "space")
    grad_weight = summed * voxel_total ** (-0.5)
    full_kernel = lax.all_gather(weight, "chan", axis=1, tiled=True)
    column_start = lax.axis_index("chan") * narrow
    my_kernel = lax.dynamic_slice_in_dim(full_kernel, column_start, narrow, 2)
    grad_padded = assemble(grad_views[0], grad_views[1], grad_views[2], neighbours, own_start)
    backward = jnp.zeros((brick_count, narrow, flat_width), jnp.float32)
    for step_x in range(3):
        for step_y in range(3):
            for step_z in range(3):
                index_k = 9 * step_x + 3 * step_y + step_z
                offset = 100 * step_x + 10 * step_y + step_z
                window = grad_padded[:, :, offset : offset + flat_width]
                backward = backward + jnp.einsum(
                    "oc,ron->rcn",
                    my_kernel[26 - index_k],
                    window,
                    preferred_element_type=jnp.float32,
                )
    grad_input = from_padded_grid(backward).astype(jnp.bfloat16)
    return (output, grad_input, grad_weight)


def solution(mesh):
    in_specs = (
        P("space", "chan", None),
        P(None, "chan", None),
        P("space", "chan", None),
        P("space", None),
    )
    out_specs = (P("space", "chan", None), P("space", "chan", None), P(None, "chan", None))
    return jax.shard_map(body, mesh=mesh, in_specs=in_specs, out_specs=out_specs, check_vma=False)
```

profile of v0, /device:TPU:1, one launch (start us, length us, event | category | flops | bytes accessed | tf_op | source)
XLA Modules:
  0.0 693.3 jit_solution(12567140329959811649)
XLA Ops:
  7.2 13.3 %all-gather = bf16[8,64,512]{2,1,0:T(8,128)(2,1)} all-gather(bf16[8,16,512]{2,1,0:T(8,128)(2,1)} %param.84), channel_id=2, replica_groups=mesh['space'=128,'chan'=4] {'chan'}, dimensions={1}, use_global_device_ids=true | all-gather | bytes 655360 | tf_op jit(solution)/shard_map/all_gather | solution.py:72
  20.6 6.3 collective-permute-start
  26.9 4.9 collective-permute-start.1
  31.8 13.0 %all-gather.1 = bf16[8,64,512]{2,1,0:T(8,128)(2,1)} all-gather(bf16[8,16,512]{2,1,0:T(8,128)(2,1)} %param.86), channel_id=3, replica_groups=mesh['space'=128,'chan'=4] {'chan'}, dimensions={1}, use_global_device_ids=true | all-gather | bytes 655360 | tf_op jit(solution)/shard_map/all_gather | solution.py:72
  44.8 1.9 collective-permute-start.2
  46.8 3.2 collective-permute-start.3
  101.6 1.8 gather_fusion.16
  106.0 2.5 gather_fusion.18
  113.7 2.5 gather_fusion.22
  119.2 2.0 gather_fusion.24
  121.2 2.4 gather_fusion.72
  128.4 2.5 gather_fusion.26
  130.9 2.5 gather_fusion.74
  145.5 2.5 gather_fusion.30
  148.0 2.5 gather_fusion.78
  158.1 4.0 gather_fusion
  162.1 4.5 multiply_bitcast_fusion
  169.6 12.5 %all_gather.11 = bf16[27,64,64]{2,1,0:T(8,128)(2,1)} all-gather(bf16[27,16,64]{2,1,0:T(8,128)(2,1)S(1)} %copy-done.25), channel_id=1, replica_groups=mesh['space'=128,'chan'=4] {'chan'}, dimensions={1}, use_global_device_ids=true | all-gather | bytes 276480 | tf_op jit(solution)/shard_map/all_gather | solution.py:136
  229.9 1.8 broadcast_select_fusion.34
  249.5 2.2 gather_fusion.8
  251.7 2.2 gather_fusion.56
  260.4 1.9 slice_select_fusion.1
  308.5 2.6 bitcast_dynamic-update-slice_fusion
  322.6 5.1 gather_fusion.47
  327.7 2.1 copy.219
  346.6 9.2 %gather_fusion.95 = bf16[1000,8,64]{2,1,0:T(8,128)(2,1)} fusion(bf16[8,64,1000]{1,0,2:T(8,128)(2,1)} %get-tuple-element.60, s32[1024]{0:T(1024)S(1)} %get-tuple-element.187), kind=kCustom, calls=%fused_computation.94.clone | custom fusion | bytes 2052000 | tf_op jit(solution)/shard_map/jit(_take)/gather | solution.py:96
  355.8 2.7 copy.248
  383.0 1.9 copy.250
  385.0 1.8 gather_fusion.96
  388.1 1.9 copy.220
  390.0 1.8 gather_fusion.48
  393.2 291.2 %all-reduce.10.cloned.1.call-done = f32[27,16,64]{2,1,0:T(8,128)} async-done(((f32[27,16,64]{2,1,0:T(8,128)}), f32[27,16,64]{2,1,0:T(8,128)}) %all-reduce.10.cloned.1.call-update) | async-done | bytes 110608 | tf_op jit(solution)/shard_map/psum | solution.py:134
  (526 shorter events, 264.0 us)
Async XLA Ops:
  7.2 48.6 %copy-start = (s32[8,27]{1,0:T(8,128)S(1)}, s32[8,27]{1,0:T(8,128)}, u32[]{:S(2)}) copy-start(s32[8,27]{1,0:T(8,128)} %param.87) | copy-start | bytes 2596
  7.2 677.2 %all-reduce.10.cloned.1.call-start = ((), (), s32[]{:S(2)}) async-start(), calls=%async_computation | async-start | bytes 442368 | tf_op jit(solution)/shard_map/psum | solution.py:134
  20.6 162.6 %collective-permute-start = (bf16[1,8,64,512]{3,2,1,0:T(8,128)(2,1)}, bf16[1,8,64,512]{3,2,1,0:T(8,128)(2,1)}, u32[]{:S(2)}, u32[]{:S(2)}) collective-permute-start(bf16[1,8,64,512]{3,2,1,0:T(8,128)(2,1)} %bitcast), channel_id=1, source_target_pairs={{0,4},{4,8},{8,12},{12,16},{16,20},{20,24},{24,28},{28,32},{32,36}... | collective-permute-start | bytes 1572872 | tf_op jit(solution)/shard_map/ppermute | solution.py:14
  26.9 177.4 %collective-permute-start.1 = (bf16[1,8,64,512]{3,2,1,0:T(8,128)(2,1)}, bf16[1,8,64,512]{3,2,1,0:T(8,128)(2,1)}, u32[]{:S(2)}, u32[]{:S(2)}) collective-permute-start(bf16[1,8,64,512]{3,2,1,0:T(8,128)(2,1)} %bitcast), channel_id=1, source_target_pairs={{4,0},{8,4},{12,8},{16,12},{20,16},{24,20},{28,24},{32,28},{36,32}... | collective-permute-start | bytes 1572872 | tf_op jit(solution)/shard_map/ppermute | solution.py:14
  44.8 137.3 %collective-permute-start.2 = (bf16[1,8,64,512]{3,2,1,0:T(8,128)(2,1)}, bf16[1,8,64,512]{3,2,1,0:T(8,128)(2,1)}, u32[]{:S(2)}, u32[]{:S(2)}) collective-permute-start(bf16[1,8,64,512]{3,2,1,0:T(8,128)(2,1)} %bitcast.89), channel_id=1, source_target_pairs={{0,4},{4,8},{8,12},{12,16},{16,20},{20,24},{24,28},{28,32},{32,36}... | collective-permute-start | bytes 1572872 | tf_op jit(solution)/shard_map/ppermute | solution.py:14
  46.8 158.4 %collective-permute-start.3 = (bf16[1,8,64,512]{3,2,1,0:T(8,128)(2,1)}, bf16[1,8,64,512]{3,2,1,0:T(8,128)(2,1)}, u32[]{:S(2)}, u32[]{:S(2)}) collective-permute-start(bf16[1,8,64,512]{3,2,1,0:T(8,128)(2,1)} %bitcast.89), channel_id=1, source_target_pairs={{4,0},{8,4},{12,8},{16,12},{20,16},{24,20},{28,24},{32,28},{36,32}... | collective-permute-start | bytes 1572872 | tf_op jit(solution)/shard_map/ppermute | solution.py:14
  52.5 35.4 %copy-start.41 = (s32[8]{0:T(128)}, s32[8]{0:T(128)S(1)}, u32[]{:S(2)}) copy-start(s32[8]{0:T(128)S(1)} %get-tuple-element.53) | copy-start | bytes 100
  56.2 99.3 %copy-start.59 = (s32[8]{0:T(128)}, s32[8]{0:T(128)S(1)}, u32[]{:S(2)}) copy-start(s32[8]{0:T(128)S(1)} %get-tuple-element.40) | copy-start | bytes 100
  138.4 12.0 %copy-start.2 = (bf16[8,64,512]{2,1,0:T(8,128)(2,1)S(1)}, bf16[8,64,512]{2,1,0:T(8,128)(2,1)}, u32[]{:S(2)}) copy-start(bf16[8,64,512]{2,1,0:T(8,128)(2,1)} %gather_fusion.31) | copy-start | bytes 1572868
  138.4 12.0 %copy-start.3 = (bf16[8,64,512]{2,1,0:T(8,128)(2,1)S(1)}, bf16[8,64,512]{2,1,0:T(8,128)(2,1)}, u32[]{:S(2)}) copy-start(bf16[8,64,512]{2,1,0:T(8,128)(2,1)} %gather_fusion.79) | copy-start | bytes 1572868
  150.7 11.4 %copy-start.30 = (bf16[896]{0:T(1024)(128)(2,1)S(1)}, bf16[896]{0:T(1024)(128)(2,1)}, u32[]{:S(2)}) copy-start(bf16[896]{0:T(1024)(128)(2,1)} %constant.267) | copy-start | bytes 5380
  208.8 14.8 %copy-start.48 = (pred[8]{0:T(512)(128)(4,1)S(1)}, pred[8]{0:T(512)(128)(4,1)}, u32[]{:S(2)}) copy-start(pred[8]{0:T(512)(128)(4,1)} %get-tuple-element.184) | copy-start | bytes 28
  212.3 13.1 %copy-start.46 = (pred[8]{0:T(512)(128)(4,1)S(1)}, pred[8]{0:T(512)(128)(4,1)}, u32[]{:S(2)}) copy-start(pred[8]{0:T(512)(128)(4,1)} %get-tuple-element.185) | copy-start | bytes 28
  215.0 13.0 %copy-start.47 = (pred[8]{0:T(512)(128)(4,1)S(1)}, pred[8]{0:T(512)(128)(4,1)}, u32[]{:S(2)}) copy-start(pred[8]{0:T(512)(128)(4,1)} %get-tuple-element.183) | copy-start | bytes 28
  216.4 13.5 %copy-start.45 = (pred[8]{0:T(512)(128)(4,1)S(1)}, pred[8]{0:T(512)(128)(4,1)}, u32[]{:S(2)}) copy-start(pred[8]{0:T(512)(128)(4,1)} %get-tuple-element.182) | copy-start | bytes 28
  225.4 19.0 %copy-start.44 = (pred[8]{0:T(512)(128)(4,1)S(1)}, pred[8]{0:T(512)(128)(4,1)}, u32[]{:S(2)}) copy-start(pred[8]{0:T(512)(128)(4,1)} %get-tuple-element.181) | copy-start | bytes 28
  229.8 24.0 %copy-start.20 = (bf16[8,64,64]{2,1,0:T(8,128)(2,1)S(1)}, bf16[8,64,64]{2,1,0:T(8,128)(2,1)}, u32[]{:S(2)}) copy-start(bf16[8,64,64]{2,1,0:T(8,128)(2,1)} %gather_fusion.9) | copy-start | bytes 196612
  229.8 24.0 %copy-start.43 = (pred[8]{0:T(512)(128)(4,1)S(1)}, pred[8]{0:T(512)(128)(4,1)}, u32[]{:S(2)}) copy-start(pred[8]{0:T(512)(128)(4,1)} %get-tuple-element.180) | copy-start | bytes 28
  242.9 21.4 %copy-start.19 = (bf16[8,64,64]{2,1,0:T(8,128)(2,1)S(1)}, bf16[8,64,64]{2,1,0:T(8,128)(2,1)}, u32[]{:S(2)}) copy-start(bf16[8,64,64]{2,1,0:T(8,128)(2,1)} %gather_fusion.60) | copy-start | bytes 196612
  242.9 21.4 %copy-start.35 = (pred[8]{0:T(512)(128)(4,1)S(1)}, pred[8]{0:T(512)(128)(4,1)}, u32[]{:S(2)}) copy-start(pred[8]{0:T(512)(128)(4,1)} %get-tuple-element.177) | copy-start | bytes 28
  251.7 18.1 %copy-start.34 = (pred[8]{0:T(512)(128)(4,1)S(1)}, pred[8]{0:T(512)(128)(4,1)}, u32[]{:S(2)}) copy-start(pred[8]{0:T(512)(128)(4,1)} %get-tuple-element.176) | copy-start | bytes 28
  260.3 13.8 %copy-start.18 = (bf16[8,64,64]{2,1,0:T(8,128)(2,1)S(1)}, bf16[8,64,64]{2,1,0:T(8,128)(2,1)}, u32[]{:S(2)}) copy-start(bf16[8,64,64]{2,1,0:T(8,128)(2,1)} %gather_fusion.82) | copy-start | bytes 196612
  260.3 13.7 %copy-start.40 = (pred[8]{0:T(512)(128)(4,1)S(1)}, pred[8]{0:T(512)(128)(4,1)}, u32[]{:S(2)}) copy-start(pred[8]{0:T(512)(128)(4,1)} %get-tuple-element.165) | copy-start | bytes 28
  281.9 13.3 %copy-start.16 = (bf16[64,8,64]{2,1,0:T(8,128)(2,1)S(1)}, bf16[64,8,64]{2,1,0:T(8,128)(2,1)}, u32[]{:S(2)}) copy-start(bf16[64,8,64]{2,1,0:T(8,128)(2,1)} %gather_fusion.8) | copy-start | bytes 196612
  281.9 13.3 %copy-start.17 = (bf16[64,8,64]{2,1,0:T(8,128)(2,1)S(1)}, bf16[64,8,64]{2,1,0:T(8,128)(2,1)}, u32[]{:S(2)}) copy-start(bf16[64,8,64]{2,1,0:T(8,128)(2,1)} %gather_fusion.56) | copy-start | bytes 196612
  281.9 13.2 %copy-start.31 = (pred[64]{0:T(512)(128)(4,1)S(1)}, pred[64]{0:T(512)(128)(4,1)}, u32[]{:S(2)}) copy-start(pred[64]{0:T(512)(128)(4,1)} %broadcast_compare_fusion.2) | copy-start | bytes 196
  282.1 13.9 %copy-start.33 = (pred[8]{0:T(512)(128)(4,1)S(1)}, pred[8]{0:T(512)(128)(4,1)}, u32[]{:S(2)}) copy-start(pred[8]{0:T(512)(128)(4,1)} %get-tuple-element.179) | copy-start | bytes 28
  282.1 15.8 %copy-start.32 = (pred[8]{0:T(512)(128)(4,1)S(1)}, pred[8]{0:T(512)(128)(4,1)}, u32[]{:S(2)}) copy-start(pred[8]{0:T(512)(128)(4,1)} %broadcast_compare_fusion.1) | copy-start | bytes 28
  284.4 24.0 %copy-start.1 = (bf16[512,8,64]{2,1,0:T(8,128)(2,1)S(1)}, bf16[512,8,64]{2,1,0:T(8,128)(2,1)}, u32[]{:S(2)}) copy-start(bf16[512,8,64]{2,1,0:T(8,128)(2,1)} %gather_fusion.72) | copy-start | bytes 1572868
  284.4 24.0 %copy-start.57 = (pred[512]{0:T(512)(128)(4,1)S(1)}, pred[512]{0:T(512)(128)(4,1)}, u32[]{:S(2)}) copy-start(pred[512]{0:T(512)(128)(4,1)} %broadcast_compare_fusion) | copy-start | bytes 1540
  308.5 12.1 %copy-start.51 = (pred[8]{0:T(512)(128)(4,1)S(1)}, pred[8]{0:T(512)(128)(4,1)}, u32[]{:S(2)}) copy-start(pred[8]{0:T(512)(128)(4,1)} %get-tuple-element.160) | copy-start | bytes 28
  308.5 13.4 %copy-start.50 = (pred[8]{0:T(512)(128)(4,1)S(1)}, pred[8]{0:T(512)(128)(4,1)}, u32[]{:S(2)}) copy-start(pred[8]{0:T(512)(128)(4,1)} %get-tuple-element.158) | copy-start | bytes 28
  (45 other events, 259.4 us)
Sparse Core Ops, SparseCore 0:
  346.7 337.6 all-reduce.9
where the time goes:
time: 703 us; the launch traced here: 693 us
  waiting for transfers between devices  291 us (41%)
  local copies, waits for them, and re-layouts  236 us (34%)
  other arithmetic  54.3 us (8%)
  matrix products  40.2 us (6%)
  blocking collectives  38.9 us (6%)
  starting transfers between devices  16.3 us (2%)
  between operations  16.1 us (2%)
    psum x1, waiting for transfers between devices, body(): summed = lax.psum(jnp.stack(kernel_terms), 'space')  291 us
    gather x54, local copies, waits for them, and re-layouts, assemble(): picked = jnp.take(sources[step_x], local_ids, axis=0)  60.5 us
    gather x38, local copies, waits for them, and re-layouts, assemble(): pieces.append(jnp.take(picked, jnp.asarray(lists[index_k]), axis=2))  54.5 us
    select_n x38, local copies, waits for them, and re-layouts, assemble(): picked = jnp.take(sources[step_x], local_ids, axis=0)  42.1 us
    unnamed x183, local copies, waits for them, and re-layouts  30.2 us
    all_gather x2, blocking collectives, spread(): entire = lax.all_gather(own_part, 'chan', axis=2, tiled=True)  26.4 us
    select_n x38, other arithmetic, assemble(): picked = jnp.take(sources[step_x], local_ids, axis=0)  23.9 us
    gather x4, local copies, waits for them, and re-layouts, assemble(): flat = jnp.take(joined, jnp.asarray(order), axis=2)  19.1 us
  transfers between devices with their start and end apart: 5, of which 1 were waited for; matrix products, arithmetic and copies ran while one was open for 27% of the time, Pallas kernels for 0%

commit v1 on v0

v1 whole, which is shorter than its diff:
```python
import functools

import jax
import jax.numpy as jnp
from jax import lax
from jax.experimental import pallas as pl
from jax.experimental.pallas import tpu as pltpu
from jax.sharding import PartitionSpec as P

MESH = pl.DeviceIdType.MESH
BRICKS = 8
HALF = 4
SHARE = 16
KERNEL_TILES = 32


def push(source, target, send_sem, recv_sem, device):
    return pltpu.make_async_remote_copy(
        src_ref=source,
        dst_ref=target,
        send_sem=send_sem,
        recv_sem=recv_sem,
        device_id=device,
        device_id_type=MESH,
    )


def gather_kernel(
    n_space, feat, cot, planes, wcut, all_feat, all_cot, all_planes, all_wcut,
    local_sem, ring_send, ring_recv, fwd_send, fwd_recv, plane_send, plane_recv, w_send, w_recv,
):
    me = lax.axis_index("chan")
    here = lax.axis_index("space")
    right, left, across = lax.rem(me + 1, 4), lax.rem(me + 3, 4), lax.rem(me + 2, 4)
    after, before = lax.rem(here + 1, n_space), lax.rem(here + n_space - 1, n_space)

    barrier = pltpu.get_barrier_semaphore()
    for other in (right, left, across):
        pl.semaphore_signal(barrier, inc=1, device_id=(here, other), device_id_type=MESH)
    for place in (after, before):
        for turn in range(4):
            pl.semaphore_signal(
                barrier, inc=1, device_id=(place, lax.rem(me + turn, 4)), device_id_type=MESH
            )
    pl.semaphore_wait(barrier, 11)

    pairs = ((feat, all_feat), (cot, all_cot))
    firsts = []
    for order in range(2):
        for tensor, (own, every) in enumerate(pairs):
            for side, peer in enumerate((right, left)):
                half = order if side == 0 else 1 - order
                rows = pl.ds(HALF * half, HALF)
                copy = push(
                    own.at[rows], every.at[me, rows],
                    ring_send.at[side, half, tensor], ring_recv.at[side, half, tensor], (here, peer),
                )
                copy.start()
                firsts.append(copy)
    others = []
    for direction, place in enumerate((after, before)):
        for turn in range(4):
            copy = push(
                planes.at[direction], all_planes.at[direction, me],
                plane_send.at[direction, turn], plane_recv.at[direction, turn],
                (place, lax.rem(me + turn, 4)),
            )
            copy.start()
            others.append((copy, direction, turn))
    weights = []
    for turn in range(1, 4):
        peer = lax.rem(me + turn, 4)
        copy = push(
            wcut.at[peer], all_wcut.at[me], w_send.at[turn - 1], w_recv.at[turn - 1], (here, peer)
        )
        copy.start()
        weights.append((copy, turn))
    locals_ = [
        pltpu.make_async_copy(feat, all_feat.at[me], local_sem.at[0]),
        pltpu.make_async_copy(cot, all_cot.at[me], local_sem.at[1]),
        pltpu.make_async_copy(wcut.at[me], all_wcut.at[me], local_sem.at[2]),
    ]
    for copy in locals_:
        copy.start()

    seconds = []
    for tensor, (own, every) in enumerate(pairs):
        for side, (source, peer) in enumerate(((left, right), (right, left))):
            half = side
            rows = pl.ds(HALF * half, HALF)
            push(
                own.at[rows], every.at[source, rows],
                ring_send.at[side, half, tensor], ring_recv.at[side, half, tensor], (here, peer),
            ).wait_recv()
            copy = push(
                every.at[source, rows], every.at[source, rows],
                fwd_send.at[side, tensor], fwd_recv.at[side, tensor], (here, peer),
            )
            copy.start()
            seconds.append(copy)
    for tensor, (own, every) in enumerate(pairs):
        for side, source in enumerate((left, right)):
            half = 1 - side
            rows = pl.ds(HALF * half, HALF)
            push(
                own.at[rows], every.at[source, rows],
                ring_send.at[side, half, tensor], ring_recv.at[side, half, tensor], (here, source),
            ).wait_recv()
            rows = pl.ds(HALF * side, HALF)
            push(
                every.at[across, rows], every.at[across, rows],
                fwd_send.at[side, tensor], fwd_recv.at[side, tensor], (here, source),
            ).wait_recv()
    for copy, direction, turn in others:
        source = lax.rem(me + 4 - turn, 4)
        push(
            planes.at[direction], all_planes.at[direction, source],
            plane_send.at[direction, turn], plane_recv.at[direction, turn], (before, source),
        ).wait_recv()
    for copy, turn in weights:
        source = lax.rem(me + 4 - turn, 4)
        push(
            wcut.at[source], all_wcut.at[source], w_send.at[turn - 1], w_recv.at[turn - 1], (here, source)
        ).wait_recv()
    for copy in locals_:
        copy.wait()
    for copy in firsts + seconds:
        copy.wait_send()
    for copy, direction, turn in others:
        copy.wait_send()
    for copy, turn in weights:
        copy.wait_send()


def conv_kernel(
    scale, table, all_feat, all_cot, all_planes, cot, weight, wback,
    out, grad_in, grad_w, bricks, prev, nxt, wt, stage, rows, acc,
):
    zero = jnp.zeros((8, 8, 128), jnp.float32)
    for u in range(8):
        bricks[BRICKS, u] = zero
    prev[BRICKS] = zero
    nxt[BRICKS] = zero
    wt[96:128, :] = jnp.zeros((32, 1152), jnp.bfloat16)
    for a in range(3):
        for j in range(9):
            k = 9 * a + j
            wt[32 * a : 32 * a + 16, 128 * j : 128 * j + 128] = weight[k]
            wt[32 * a + 16 : 32 * a + 32, 128 * j : 128 * j + 128] = wback[26 - k]

    def turn_brick(s, carry):
        both = jnp.concatenate(
            [all_feat[:, s].reshape(64, 512), all_cot[:, s].reshape(64, 512)], axis=0
        )
        bricks[s] = both.astype(jnp.float32).T.reshape(8, 8, 8, 128)
        return carry

    lax.fori_loop(0, BRICKS, turn_brick, 0)
    for direction, held in enumerate((prev, nxt)):
        for pair in range(BRICKS // 2):
            both = jnp.concatenate(
                [all_planes[direction, :, t, pair].reshape(64, 128) for t in range(2)], axis=0
            )
            held[2 * pair : 2 * pair + 2] = both.astype(jnp.float32).T.reshape(2, 8, 8, 128)

    acc[...] = jnp.zeros(acc.shape, jnp.float32)

    def one_brick(r, carry):
        def slot(i, j, k):
            named = table[r, 9 * i + 3 * j + k]
            return jnp.where(named < 0, BRICKS, jnp.bitwise_and(named, BRICKS - 1))

        for i in range(3):
            for j in range(3):
                vs = (slice(7, 8), slice(0, 8), slice(0, 1))[j]
                ys = (slice(0, 1), slice(1, 9), slice(9, 10))[j]
                ids = [slot(i, j, k) for k in range(3)]
                for u in range(8) if i == 1 else (0,):
                    x = (0, u + 1, 9)[i]
                    if i == 1:
                        low, mid, high = [bricks[s, u, vs] for s in ids]
                    else:
                        low, mid, high = [(prev, None, nxt)[i][s, vs] for s in ids]
                    w = lax.broadcasted_iota(jnp.int32, mid.shape, 1)
                    stage[0, x, ys] = pltpu.roll(jnp.where(w == 7, low, mid), 1, 1)
                    stage[1, x, ys] = mid
                    stage[2, x, ys] = pltpu.roll(jnp.where(w == 0, high, mid), 7, 1)
        for b in range(3):
            for c in range(3):
                j = 3 * b + c
                for x in range(10):
                    rows[64 * x : 64 * x + 64, 128 * j : 128 * j + 128] = (
                        stage[c, x, b : b + 8].reshape(64, 128).astype(jnp.bfloat16)
                    )
        terms = lax.dot_general(
            rows[...], wt[...], (((1,), (1,)), ((), ())), preferred_element_type=jnp.float32
        )
        turned = terms.T
        total = (
            turned[0:32, 0:512]
            + pltpu.roll(turned[32:64], 640 - 64, 1)[:, 0:512]
            + turned[64:96, 128:640]
        )
        out[r] = total[0:16].astype(jnp.bfloat16)
        grad_in[r] = total[16:32].astype(jnp.bfloat16)
        wide = jnp.concatenate(
            [cot[r].astype(jnp.float32), jnp.zeros((SHARE, 128), jnp.float32)], axis=1
        )
        lifted = jnp.concatenate([wide, pltpu.roll(wide, 64, 1), pltpu.roll(wide, 128, 1)], axis=0)
        acc[...] += jnp.dot(
            lifted.astype(jnp.bfloat16), rows[...], preferred_element_type=jnp.float32
        )
        return carry

    lax.fori_loop(0, BRICKS, one_brick, 0)
    lane = lax.broadcasted_iota(jnp.int32, (8, 128), 1)
    for a in range(3):
        for j in range(9):
            term = acc[16 * a : 16 * a + 16, 128 * j : 128 * j + 128] * scale
            grad_w[9 * a + j] = jnp.where(lane < 64, term[0:8], pltpu.roll(term[8:16], 64, 1))
    for k in range(27, KERNEL_TILES):
        grad_w[k] = jnp.zeros((8, 128), jnp.float32)


def sum_kernel(
    inner, outer, part, result, pieces, tile, blocks, whole,
    a_send, a_recv, b_send, b_recv, c_send, c_recv, local_sem,
):
    here = lax.axis_index("space")
    chan = lax.axis_index("chan")
    rank = lax.rem(here, inner)
    block = here // inner
    share = KERNEL_TILES // inner

    barrier = pltpu.get_barrier_semaphore()

    def greet(d, carry):
        peer = block * inner + lax.rem(rank + d, inner)
        pl.semaphore_signal(barrier, inc=1, device_id=(peer, chan), device_id_type=MESH)
        return carry

    lax.fori_loop(1, inner, greet, 0)
    for d in range(1, outer):
        peer = lax.rem(block + d, outer) * inner + rank
        pl.semaphore_signal(barrier, inc=1, device_id=(peer, chan), device_id_type=MESH)
    pl.semaphore_wait(barrier, inner - 1 + outer - 1)

    def scatter(d):
        to = lax.rem(rank + d, inner)
        return push(
            part.at[pl.ds(to * share, share)], pieces.at[d], a_send.at[d], a_recv.at[d],
            (block * inner + to, chan),
        )

    def start_scatter(d, carry):
        scatter(d).start()
        return carry

    def wait_scatter(d, carry):
        scatter(d).wait()
        return carry

    lax.fori_loop(1, inner, start_scatter, 0)
    pieces[0] = part[pl.ds(rank * share, share)]
    lax.fori_loop(1, inner, wait_scatter, 0)
    tile[...] = jnp.sum(pieces[...], axis=0)

    exchanges = []
    for d in range(1, outer):
        peer = lax.rem(block + d, outer)
        copy = push(
            tile, blocks.at[block], b_send.at[d - 1], b_recv.at[d - 1], (peer * inner + rank, chan)
        )
        copy.start()
        exchanges.append(copy)
    own = pltpu.make_async_copy(tile, blocks.at[block], local_sem)
    own.start()
    own.wait()
    for copy in exchanges:
        copy.wait()
    mine = pl.ds(rank * share, share)
    whole[mine] = jnp.sum(blocks[...], axis=0)

    def spread(d):
        to = lax.rem(rank + d, inner)
        return push(
            whole.at[mine], whole.at[mine], c_send.at[d], c_recv.at[d], (block * inner + to, chan)
        )

    def start_spread(d, carry):
        spread(d).start()
        return carry

    def wait_spread(d, carry):
        origin = lax.rem(rank + inner - d, inner)
        theirs = pl.ds(origin * share, share)
        push(
            whole.at[theirs], whole.at[theirs], c_send.at[d], c_recv.at[d], (block * inner + origin, chan)
        ).wait_recv()
        return carry

    def sent_spread(d, carry):
        spread(d).wait_send()
        return carry

    lax.fori_loop(1, inner, start_spread, 0)
    lax.fori_loop(1, inner, wait_spread, 0)
    lax.fori_loop(1, inner, sent_spread, 0)
    for k in range(27):
        term = whole[k]
        result[k, 0:8] = term[:, 0:64]
        result[k, 8:16] = pltpu.roll(term, 64, 1)[:, 0:64]


def body(n_space, features, weight, cotangent, neighbours):
    inner = 32 if n_space % 32 == 0 else n_space // 2
    outer = n_space // inner
    vmem = pl.BlockSpec(memory_space=pltpu.VMEM)
    anyspace = pl.BlockSpec(memory_space=pl.ANY)
    smem = pl.BlockSpec(memory_space=pltpu.SMEM)
    bf16, f32 = jnp.bfloat16, jnp.float32

    sides = []
    for lanes in (slice(448, 512), slice(0, 64)):
        both = [
            jnp.concatenate([t[0::2, :, lanes], t[1::2, :, lanes]], axis=2) for t in (features, cotangent)
        ]
        sides.append(jnp.stack(both))
    planes = jnp.stack(sides)
    wcut = weight.transpose(2, 0, 1).reshape(4, SHARE, 27 * SHARE)

    dma = pltpu.SemaphoreType.DMA
    all_feat, all_cot, all_planes, all_wcut = pl.pallas_call(
        functools.partial(gather_kernel, n_space),
        out_shape=(
            jax.ShapeDtypeStruct((4, BRICKS, SHARE, 512), bf16),
            jax.ShapeDtypeStruct((4, BRICKS, SHARE, 512), bf16),
            jax.ShapeDtypeStruct((2, 4, 2, BRICKS // 2, SHARE, 128), bf16),
            jax.ShapeDtypeStruct((4, SHARE, 27 * SHARE), bf16),
        ),
        in_specs=[anyspace] * 4,
        out_specs=(vmem,) * 4,
        scratch_shapes=[
            dma((3,)), dma((2, 2, 2)), dma((2, 2, 2)), dma((2, 2)), dma((2, 2)),
            dma((2, 4)), dma((2, 4)), dma((3,)), dma((3,)),
        ],
        compiler_params=pltpu.CompilerParams(collective_id=0, has_side_effects=True),
        name="gather",
    )(features, cotangent, planes, wcut)

    wback = all_wcut.reshape(4, SHARE, 27, SHARE).transpose(2, 1, 0, 3).reshape(27, SHARE, 64)
    wback = jnp.pad(wback, ((0, 0), (0, 0), (64, 0)))
    wfore = jnp.pad(weight, ((0, 0), (0, 0), (0, 64)))

    voxels = n_space * BRICKS * 512
    output, grad_input, part = pl.pallas_call(
        functools.partial(conv_kernel, voxels ** (-0.5)),
        out_shape=(
            jax.ShapeDtypeStruct((BRICKS, SHARE, 512), bf16),
            jax.ShapeDtypeStruct((BRICKS, SHARE, 512), bf16),
            jax.ShapeDtypeStruct((KERNEL_TILES, 8, 128), f32),
        ),
        in_specs=[smem] + [vmem] * 6,
        out_specs=(vmem,) * 3,
        scratch_shapes=[
            pltpu.VMEM((BRICKS + 1, 8, 8, 8, 128), f32),
            pltpu.VMEM((BRICKS + 1, 8, 8, 128), f32),
            pltpu.VMEM((BRICKS + 1, 8, 8, 128), f32),
            pltpu.VMEM((128, 1152), bf16),
            pltpu.VMEM((3, 10, 10, 8, 128), f32),
            pltpu.VMEM((640, 1152), bf16),
            pltpu.VMEM((48, 1152), f32),
        ],
        compiler_params=pltpu.CompilerParams(vmem_limit_bytes=48 * 2**20),
        name="conv",
    )(neighbours, all_feat, all_cot, all_planes, cotangent, wfore, wback)

    share = KERNEL_TILES // inner
    grad_weight = pl.pallas_call(
        functools.partial(sum_kernel, inner, outer),
        out_shape=jax.ShapeDtypeStruct((27, SHARE, 64), f32),
        in_specs=[vmem],
        out_specs=vmem,
        scratch_shapes=[
            pltpu.VMEM((inner, share, 8, 128), f32),
            pltpu.VMEM((share, 8, 128), f32),
            pltpu.VMEM((outer, share, 8, 128), f32),
            pltpu.VMEM((KERNEL_TILES, 8, 128), f32),
            dma((inner,)), dma((inner,)), dma((outer - 1,)), dma((outer - 1,)),
            dma((inner,)), dma((inner,)), dma(()),
        ],
        compiler_params=pltpu.CompilerParams(collective_id=1, has_side_effects=True),
        name="sum",
    )(part)
    return (output, grad_input, grad_weight)


def solution(mesh):
    in_specs = (
        P("space", "chan", None),
        P(None, "chan", None),
        P("space", "chan", None),
        P("space", None),
    )
    out_specs = (P("space", "chan", None), P("space", "chan", None), P(None, "chan", None))
    return jax.shard_map(
        functools.partial(body, mesh.shape["space"]),
        mesh=mesh, in_specs=in_specs, out_specs=out_specs, check_vma=False,
    )
```

time: 703 us -> 75.1 us (0.11); the launches traced: 693 us -> 74.8 us
  waiting for transfers between devices: 291 us -> 0 us
  local copies, waits for them, and re-layouts: 236 us -> 7.72 us
  Pallas kernels: 0 us -> 65.5 us
  other arithmetic: 54.3 us -> 0.82 us
  matrix products: 40.2 us -> 0 us
  blocking collectives: 38.9 us -> 0 us
  starting transfers between devices: 16.3 us -> 0 us
  between operations: 16.1 us -> 0.77 us
    psum x1 -> x0, waiting for transfers between devices: 291 us -> none  [body(): summed = lax.psum(jnp.stack(kernel_terms), 'space')]
    gather x99 -> x0, local copies, waits for them, and re-layouts: 142 us -> none  [the longest x54 60.5 us: assemble(): picked = jnp.take(sources[step_x], local_ids, axis=0)]
    pallas_call x0 -> x3, Pallas kernels: none -> 65.5 us  [the longest x1 31.5 us: body(): pl.pallas_call(functools.partial(sum_kernel, inner, outer), out_shape=jax...]
    select_n x52 -> x0, local copies, waits for them, and re-layouts: 52.6 us -> none  [the longest x38 42.1 us: assemble(): picked = jnp.take(sources[step_x], local_ids, axis=0)]
    dot_general x81 -> x0, matrix products: 40.2 us -> none  [the longest x27 14.1 us: body(): jnp.einsum('oc,ron->rcn', my_kernel[26 - index_k], window, preferred_elem...]
    all_gather x3 -> x0, blocking collectives: 38.9 us -> none  [the longest x2 26.4 us: spread(): entire = lax.all_gather(own_part, 'chan', axis=2, tiled=True)]
    unnamed x183 -> x17, local copies, waits for them, and re-layouts: 30.2 us -> 3.5 us
    select_n x42 -> x0, other arithmetic: 26.3 us -> none  [the longest x38 23.9 us: assemble(): picked = jnp.take(sources[step_x], local_ids, axis=0)]
  transfers between devices with their start and end apart: 5 -> 0, of which waited for: 1 -> 0; matrix products, arithmetic and copies ran while one was open for 27% -> 0% of each run, Pallas kernels for 0% -> 0%
where the time goes in v1:
time: 75.1 us; the launch traced here: 74.8 us
  Pallas kernels  65.5 us (87%)
  local copies, waits for them, and re-layouts  7.72 us (10%)
  other arithmetic  0.82 us (1%)
  between operations  0.77 us (1%)
    pallas_call x1, Pallas kernels, body(): pl.pallas_call(functools.partial(sum_kernel, inner, outer), out_shape=jax...  31.5 us
    pallas_call x1, Pallas kernels, body(): pl.pallas_call(functools.partial(gather_kernel, n_space), out_shape=(jax....  24.2 us
    pallas_call x1, Pallas kernels, body(): pl.pallas_call(functools.partial(conv_kernel, voxels ** (-0.5)), out_shap...  9.75 us
    unnamed x17, local copies, waits for them, and re-layouts  3.5 us
    reshape x2, local copies, waits for them, and re-layouts, body(): all_wcut.reshape(4, SHARE, 27, SHARE).transpose(2, 1, 0, 3)  1.54 us

profile of v1, /device:TPU:1, one launch (start us, length us, event | category | flops | bytes accessed | tf_op | source)
XLA Modules:
  0.0 74.8 jit_solution(16815897714571465081)
XLA Ops:
  0.6 0.0 copy-start
  0.6 0.9 %fusion = (bf16[4,16,64]{2,1,0:T(8,128)(2,1)S(1)}, bf16[4,16,64]{2,1,0:T(8,128)(2,1)S(1)}, bf16[4,16,64]{2,1,0:T(8,128)(2,1)S(1)}, bf16[4,16,64]{2,1,0:T(8,128)(2,1)S(1)}) fusion(bf16[8,16,512]{2,1,0:T(8,128)(2,1)} %feat.1), kind=kLoop, calls=%fused_computation.7 | loop fusion | bytes 65536 | tf_op jit(solution)/shard_map/slice | solution.py:326
  1.5 0.1 maximum_bitcast_fusion.2
  1.6 0.0 copy-done
  1.6 0.1 fusion.1
  1.7 0.1 maximum_bitcast_fusion.3
  1.8 0.0 copy-start.7
  1.8 0.6 pad_maximum_fusion.planes
  2.5 0.2 copy-done.7
  2.7 0.2 reshape.15
  2.9 0.9 %copy.9.wcut = bf16[4,16,432]{2,1,0:T(8,128)(2,1)} copy(bf16[4,16,432]{1,0,2:T(4,128)(2,1)S(1)} %reshape.15) | data formatting | bytes 110592 | tf_op jit(solution)/shard_map/reshape | solution.py:330
  3.8 24.2 %gather.1 = (bf16[4,8,16,512]{3,2,1,0:T(8,128)(2,1)}, bf16[4,8,16,512]{3,2,1,0:T(8,128)(2,1)}, bf16[2,4,2,4,16,128]{5,4,3,2,1,0:T(8,128)(2,1)}, bf16[4,16,432]{2,1,0:T(8,128)(2,1)}) custom-call(bf16[8,16,512]{2,1,0:T(8,128)(2,1)} %feat.1, bf16[8,16,512]{2,1,0:T(8,128)(2,1)} %cot.3, bf16[2,2,4,16,128]{4,3,2,1,0:T(8,128)(2,1)} %pad_maximum_fusion.planes, ...), custom_call_target="tpu_custom_call" | custom-call | tf_op jit(solution)/shard_map/gather/pallas_call | solution.py:333
  28.1 1.3 %reshape.16 = bf16[4,16,27,16]{3,2,1,0:T(8,128)(2,1)S(1)} reshape(bf16[4,16,432]{2,1,0:T(8,128)(2,1)} %get-tuple-element.13) | data formatting | bytes 110592 | tf_op jit(solution)/shard_map/reshape | solution.py:351
  29.4 0.0 copy-start.3
  29.4 0.0 copy-start.4
  29.4 0.5 copy.10
  29.9 0.0 copy-start.2
  29.9 0.2 copy.11
  30.1 0.1 pad.9.wback
  30.2 0.0 copy-start.1
  30.3 0.0 copy-start.6
  30.3 0.2 copy-done.3
  30.5 0.1 copy-done.4
  30.5 0.5 copy-done.2
  31.0 0.2 copy-done.1
  31.2 0.0 copy-done.6
  31.3 9.7 %conv.1 = (bf16[8,16,512]{2,1,0:T(8,128)(2,1)}, bf16[8,16,512]{2,1,0:T(8,128)(2,1)}, f32[32,8,128]{2,1,0:T(8,128)S(1)}) custom-call(s32[8,27]{1,0:T(8,128)S(1)} %copy-done.6, bf16[4,8,16,512]{3,2,1,0:T(8,128)(2,1)S(1)} %copy-done.2, bf16[4,8,16,512]{3,2,1,0:T(8,128)(2,1)S(1)} %copy-done.3, bf16[2,4,2,4,16,128]{5,4,3,2,1,0:T(8,128)(2,1)S(1)} %copy-done.4, ...), custom_call_target="tpu_custom_call" | custom-call | tf_op jit(solution)/shard_map/conv/pallas_call | solution.py:356
  41.0 0.0 copy-start.5
  41.0 0.7 copy-done.5
  41.7 31.5 %sum.1 = f32[27,16,64]{2,1,0:T(8,128)} custom-call(f32[32,8,128]{2,1,0:T(8,128)} %copy-done.5), custom_call_target="tpu_custom_call" | custom-call | tf_op jit(solution)/shard_map/sum/pallas_call | solution.py:379
  73.2 1.6 %copy.13 = f32[27,16,64]{2,1,0:T(8,128)} copy(f32[27,16,64]{2,1,0:T(8,128)} %sum.1) | data formatting | bytes 221184
  (3 shorter events, 0.0 us)
Async XLA Ops:
  0.6 1.0 %copy-start = (bf16[8,16,512]{2,1,0:T(8,128)(2,1)S(1)}, bf16[8,16,512]{2,1,0:T(8,128)(2,1)}, u32[]{:S(2)}) copy-start(bf16[8,16,512]{2,1,0:T(8,128)(2,1)} %cot.3) | copy-start | bytes 393220
  1.8 0.9 %copy-start.7 = (bf16[27,16,64]{2,1,0:T(8,128)(2,1)S(1)}, bf16[27,16,64]{2,1,0:T(8,128)(2,1)}, u32[]{:S(2)}) copy-start(bf16[27,16,64]{2,1,0:T(8,128)(2,1)} %param.5) | copy-start | bytes 165892
  29.4 1.0 %copy-start.3 = (bf16[4,8,16,512]{3,2,1,0:T(8,128)(2,1)S(1)}, bf16[4,8,16,512]{3,2,1,0:T(8,128)(2,1)}, u32[]{:S(2)}) copy-start(bf16[4,8,16,512]{3,2,1,0:T(8,128)(2,1)} %get-tuple-element.11.all_cot) | copy-start | bytes 1572868
  29.4 1.1 %copy-start.4 = (bf16[2,4,2,4,16,128]{5,4,3,2,1,0:T(8,128)(2,1)S(1)}, bf16[2,4,2,4,16,128]{5,4,3,2,1,0:T(8,128)(2,1)}, u32[]{:S(2)}) copy-start(bf16[2,4,2,4,16,128]{5,4,3,2,1,0:T(8,128)(2,1)} %get-tuple-element.12.all_planes) | copy-start | bytes 786436
  29.9 1.1 %copy-start.2 = (bf16[4,8,16,512]{3,2,1,0:T(8,128)(2,1)S(1)}, bf16[4,8,16,512]{3,2,1,0:T(8,128)(2,1)}, u32[]{:S(2)}) copy-start(bf16[4,8,16,512]{3,2,1,0:T(8,128)(2,1)} %get-tuple-element.10.all_feat) | copy-start | bytes 1572868
  30.2 1.0 %copy-start.1 = (bf16[8,16,512]{2,1,0:T(8,128)(2,1)S(1)}, bf16[8,16,512]{2,1,0:T(8,128)(2,1)}, u32[]{:S(2)}) copy-start(bf16[8,16,512]{2,1,0:T(8,128)(2,1)} %cot.3) | copy-start | bytes 393220
  30.3 1.0 %copy-start.6 = (s32[8,27]{1,0:T(8,128)S(1)}, s32[8,27]{1,0:T(8,128)}, u32[]{:S(2)}) copy-start(s32[8,27]{1,0:T(8,128)} %table.1) | copy-start | bytes 2596
  41.0 0.7 copy-start.5

commit v2 on v1

--- a/solution.py
+++ b/solution.py
@@ -132,21 +132,28 @@
         copy.wait_send()
 
 
-def conv_kernel(
-    scale, table, all_feat, all_cot, all_planes, cot, weight, wback,
-    out, grad_in, grad_w, bricks, prev, nxt, wt, stage, rows, acc,
+def assemble_all(
+    scale, table, all_feat, all_cot, all_planes, all_wcut, cot, weight, bricks, prev, nxt, wt, stage, rows, acc, part
 ):
     zero = jnp.zeros((8, 8, 128), jnp.float32)
     for u in range(8):
         bricks[BRICKS, u] = zero
     prev[BRICKS] = zero
     nxt[BRICKS] = zero
-    wt[96:128, :] = jnp.zeros((32, 1152), jnp.bfloat16)
+    wt[...] = jnp.zeros((128, 1152), jnp.bfloat16)
+    lane = lax.broadcasted_iota(jnp.int32, (SHARE, 128), 1)
     for a in range(3):
         for j in range(9):
             k = 9 * a + j
-            wt[32 * a : 32 * a + 16, 128 * j : 128 * j + 128] = weight[k]
-            wt[32 * a + 16 : 32 * a + 32, 128 * j : 128 * j + 128] = wback[26 - k]
+            wt[32 * a : 32 * a + 16, 128 * j : 128 * j + 64] = weight[k]
+            back = 26 - k
+            block = jnp.zeros((SHARE, 128), jnp.float32)
+            for p in range(4):
+                start = 64 + SHARE * p
+                piece = all_wcut[p, :, 128 * (back // 8) : 128 * (back // 8) + 128].astype(jnp.float32)
+                piece = pltpu.roll(piece, (start - SHARE * (back % 8)) % 128, 1)
+                block = jnp.where((lane >= start) & (lane < start + SHARE), piece, block)
+            wt[32 * a + 16 : 32 * a + 32, 128 * j : 128 * j + 128] = block.astype(jnp.bfloat16)
 
     def turn_brick(s, carry):
         both = jnp.concatenate(
@@ -189,11 +196,32 @@
             for c in range(3):
                 j = 3 * b + c
                 for x in range(10):
-                    rows[64 * x : 64 * x + 64, 128 * j : 128 * j + 128] = (
+                    rows[r, 64 * x : 64 * x + 64, 128 * j : 128 * j + 128] = (
                         stage[c, x, b : b + 8].reshape(64, 128).astype(jnp.bfloat16)
                     )
+        wide = jnp.concatenate(
+            [cot[r].astype(jnp.float32), jnp.zeros((SHARE, 128), jnp.float32)], axis=1
+        )
+        lifted = jnp.concatenate([wide, pltpu.roll(wide, 64, 1), pltpu.roll(wide, 128, 1)], axis=0)
+        acc[...] += jnp.dot(
+            lifted.astype(jnp.bfloat16), rows[r], preferred_element_type=jnp.float32
+        )
+        return carry
+
+    lax.fori_loop(0, BRICKS, one_brick, 0)
+    lane = lax.broadcasted_iota(jnp.int32, (8, 128), 1)
+    for a in range(3):
+        for j in range(9):
+            term = acc[16 * a : 16 * a + 16, 128 * j : 128 * j + 128] * scale
+            part[9 * a + j] = jnp.where(lane < 64, term[0:8], pltpu.roll(term[8:16], 64, 1))
+    for k in range(27, KERNEL_TILES):
+        part[k] = jnp.zeros((8, 128), jnp.float32)
+
+
+def convolve(first, last, rows, wt, out, grad_in):
+    def one_brick(r, carry):
         terms = lax.dot_general(
-            rows[...], wt[...], (((1,), (1,)), ((), ())), preferred_element_type=jnp.float32
+            rows[r], wt[...], (((1,), (1,)), ((), ())), preferred_element_type=jnp.float32
         )
         turned = terms.T
         total = (
@@ -203,28 +231,16 @@
         )
         out[r] = total[0:16].astype(jnp.bfloat16)
         grad_in[r] = total[16:32].astype(jnp.bfloat16)
-        wide = jnp.concatenate(
-            [cot[r].astype(jnp.float32), jnp.zeros((SHARE, 128), jnp.float32)], axis=1
-        )
-        lifted = jnp.concatenate([wide, pltpu.roll(wide, 64, 1), pltpu.roll(wide, 128, 1)], axis=0)
-        acc[...] += jnp.dot(
-            lifted.astype(jnp.bfloat16), rows[...], preferred_element_type=jnp.float32
-        )
-        return carry
-
-    lax.fori_loop(0, BRICKS, one_brick, 0)
-    lane = lax.broadcasted_iota(jnp.int32, (8, 128), 1)
-    for a in range(3):
-        for j in range(9):
-            term = acc[16 * a : 16 * a + 16, 128 * j : 128 * j + 128] * scale
-            grad_w[9 * a + j] = jnp.where(lane < 64, term[0:8], pltpu.roll(term[8:16], 64, 1))
-    for k in range(27, KERNEL_TILES):
-        grad_w[k] = jnp.zeros((8, 128), jnp.float32)
-
-
-def sum_kernel(
-    inner, outer, part, result, pieces, tile, blocks, whole,
-    a_send, a_recv, b_send, b_recv, c_send, c_recv, local_sem,
+        return carry
+
+    lax.fori_loop(first, last, one_brick, 0)
+
+
+def conv_kernel(
+    inner, outer, scale, table, all_feat, all_cot, all_planes, all_wcut, cot, weight,
+    out, grad_in, result,
+    bricks, prev, nxt, wt, stage, rows, acc, part, pieces, tile, blocks, whole,
+    a_send, a_recv, b_send, b_recv, c_send, c_recv,
 ):
     here = lax.axis_index("space")
     chan = lax.axis_index("chan")
@@ -243,6 +259,10 @@
     for d in range(1, outer):
         peer = lax.rem(block + d, outer) * inner + rank
         pl.semaphore_signal(barrier, inc=1, device_id=(peer, chan), device_id_type=MESH)
+    assemble_all(
+        scale, table, all_feat, all_cot, all_planes, all_wcut, cot, weight,
+        bricks, prev, nxt, wt, stage, rows, acc, part,
+    )
     pl.semaphore_wait(barrier, inner - 1 + outer - 1)
 
     def scatter(d):
@@ -262,6 +282,7 @@
 
     lax.fori_loop(1, inner, start_scatter, 0)
     pieces[0] = part[pl.ds(rank * share, share)]
+    convolve(0, BRICKS // 2, rows, wt, out, grad_in)
     lax.fori_loop(1, inner, wait_scatter, 0)
     tile[...] = jnp.sum(pieces[...], axis=0)
 
@@ -273,9 +294,8 @@
         )
         copy.start()
         exchanges.append(copy)
-    own = pltpu.make_async_copy(tile, blocks.at[block], local_sem)
-    own.start()
-    own.wait()
+    blocks[block] = tile[...]
+    convolve(BRICKS // 2, BRICKS, rows, wt, out, grad_in)
     for copy in exchanges:
         copy.wait()
     mine = pl.ds(rank * share, share)
@@ -328,6 +348,7 @@
         sides.append(jnp.stack(both))
     planes = jnp.stack(sides)
     wcut = weight.transpose(2, 0, 1).reshape(4, SHARE, 27 * SHARE)
+    wcut = jnp.pad(wcut, ((0, 0), (0, 0), (0, 512 - 27 * SHARE)))
 
     dma = pltpu.SemaphoreType.DMA
     all_feat, all_cot, all_planes, all_wcut = pl.pallas_call(
@@ -336,7 +357,7 @@
             jax.ShapeDtypeStruct((4, BRICKS, SHARE, 512), bf16),
             jax.ShapeDtypeStruct((4, BRICKS, SHARE, 512), bf16),
             jax.ShapeDtypeStruct((2, 4, 2, BRICKS // 2, SHARE, 128), bf16),
-            jax.ShapeDtypeStruct((4, SHARE, 27 * SHARE), bf16),
+            jax.ShapeDtypeStruct((4, SHARE, 512), bf16),
         ),
         in_specs=[anyspace] * 4,
         out_specs=(vmem,) * 4,
@@ -348,17 +369,14 @@
         name="gather",
     )(features, cotangent, planes, wcut)
 
-    wback = all_wcut.reshape(4, SHARE, 27, SHARE).transpose(2, 1, 0, 3).reshape(27, SHARE, 64)
-    wback = jnp.pad(wback, ((0, 0), (0, 0), (64, 0)))
-    wfore = jnp.pad(weight, ((0, 0), (0, 0), (0, 64)))
-
     voxels = n_space * BRICKS * 512
-    output, grad_input, part = pl.pallas_call(
-        functools.partial(conv_kernel, voxels ** (-0.5)),
+    share = KERNEL_TILES // inner
+    output, grad_input, grad_weight = pl.pallas_call(
+        functools.partial(conv_kernel, inner, outer, voxels ** (-0.5)),
         out_shape=(
             jax.ShapeDtypeStruct((BRICKS, SHARE, 512), bf16),
             jax.ShapeDtypeStruct((BRICKS, SHARE, 512), bf16),
-            jax.ShapeDtypeStruct((KERNEL_TILES, 8, 128), f32),
+            jax.ShapeDtypeStruct((27, SHARE, 64), f32),
         ),
         in_specs=[smem] + [vmem] * 6,
         out_specs=(vmem,) * 3,
@@ -368,30 +386,21 @@
             pltpu.VMEM((BRICKS + 1, 8, 8, 128), f32),
             pltpu.VMEM((128, 1152), bf16),
             pltpu.VMEM((3, 10, 10, 8, 128), f32),
-            pltpu.VMEM((640, 1152), bf16),
+            pltpu.VMEM((BRICKS, 640, 1152), bf16),
             pltpu.VMEM((48, 1152), f32),
-        ],
-        compiler_params=pltpu.CompilerParams(vmem_limit_bytes=48 * 2**20),
-        name="conv",
-    )(neighbours, all_feat, all_cot, all_planes, cotangent, wfore, wback)
-
-    share = KERNEL_TILES // inner
-    grad_weight = pl.pallas_call(
-        functools.partial(sum_kernel, inner, outer),
-        out_shape=jax.ShapeDtypeStruct((27, SHARE, 64), f32),
-        in_specs=[vmem],
-        out_specs=vmem,
-        scratch_shapes=[
+            pltpu.VMEM((KERNEL_TILES, 8, 128), f32),
             pltpu.VMEM((inner, share, 8, 128), f32),
             pltpu.VMEM((share, 8, 128), f32),
             pltpu.VMEM((outer, share, 8, 128), f32),
             pltpu.VMEM((KERNEL_TILES, 8, 128), f32),
             dma((inner,)), dma((inner,)), dma((outer - 1,)), dma((outer - 1,)),
-            dma((inner,)), dma((inner,)), dma(()),
+            dma((inner,)), dma((inner,)),
         ],
-        compiler_params=pltpu.CompilerParams(collective_id=1, has_side_effects=True),
-        name="sum",
-    )(part)
+        compiler_params=pltpu.CompilerParams(
+            collective_id=1, has_side_effects=True, vmem_limit_bytes=48 * 2**20
+        ),
+        name="conv",
+    )(neighbours, all_feat, all_cot, all_planes, all_wcut, cotangent, weight)
     return (output, grad_input, grad_weight)
 
 

time: 75.1 us -> 68.1 us (0.907)
  Pallas kernels: 65.5 us -> 57.3 us
  local copies, waits for them, and re-layouts: 7.72 us -> 8.88 us
    pallas_call x2 -> x1, Pallas kernels: 41.2 us -> 33 us  [body(): pl.pallas_call(functools.partial(conv_kernel, inner, outer, voxels ** (-0...]
    unnamed x17 -> x19, local copies, waits for them, and re-layouts: 3.5 us -> 6.79 us
    reshape x2 -> x0, local copies, waits for them, and re-layouts: 1.54 us -> none  [body(): all_wcut.reshape(4, SHARE, 27, SHARE).transpose(2, 1, 0, 3)]
where the time goes in v2:
time: 68.1 us; the launch traced here: 67.8 us
  Pallas kernels  57.3 us (84%)
  local copies, waits for them, and re-layouts  8.88 us (13%)
  other arithmetic  0.82 us (1%)
  between operations  0.73 us (1%)
    pallas_call x1, Pallas kernels, body(): pl.pallas_call(functools.partial(conv_kernel, inner, outer, voxels ** (-0...  33 us
    pallas_call x1, Pallas kernels, body(): pl.pallas_call(functools.partial(gather_kernel, n_space), out_shape=(jax....  24.4 us
    unnamed x19, local copies, waits for them, and re-layouts  6.79 us

profile of v2, /device:TPU:1, one launch (start us, length us, event | category | flops | bytes accessed | tf_op | source)
XLA Modules:
  0.0 67.8 jit_solution(9197606113113988174)
XLA Ops:
  0.6 0.0 copy-start
  0.6 0.9 %fusion = (bf16[4,16,64]{2,1,0:T(8,128)(2,1)S(1)}, bf16[4,16,64]{2,1,0:T(8,128)(2,1)S(1)}, bf16[4,16,64]{2,1,0:T(8,128)(2,1)S(1)}, bf16[4,16,64]{2,1,0:T(8,128)(2,1)S(1)}) fusion(bf16[8,16,512]{2,1,0:T(8,128)(2,1)} %feat.1), kind=kLoop, calls=%fused_computation.7 | loop fusion | bytes 65536 | tf_op jit(solution)/shard_map/slice | solution.py:346
  1.5 0.1 maximum_bitcast_fusion.2
  1.6 0.0 copy-done
  1.6 0.1 fusion.1
  1.7 0.1 maximum_bitcast_fusion.3
  1.8 0.0 copy-start.4
  1.8 0.6 pad_maximum_fusion.planes
  2.5 0.2 copy-done.4
  2.7 0.2 reshape.9
  2.9 0.2 copy.8
  3.2 0.7 pad.4.wcut
  3.8 0.0 copy-start.1
  3.9 24.4 %gather.1 = (bf16[4,8,16,512]{3,2,1,0:T(8,128)(2,1)}, bf16[4,8,16,512]{3,2,1,0:T(8,128)(2,1)}, bf16[2,4,2,4,16,128]{5,4,3,2,1,0:T(8,128)(2,1)}, bf16[4,16,512]{2,1,0:T(8,128)(2,1)}) custom-call(bf16[8,16,512]{2,1,0:T(8,128)(2,1)} %feat.1, bf16[8,16,512]{2,1,0:T(8,128)(2,1)} %cot.3, bf16[2,2,4,16,128]{4,3,2,1,0:T(8,128)(2,1)} %pad_maximum_fusion.planes, ...), custom_call_target="tpu_custom_call" | custom-call | tf_op jit(solution)/shard_map/gather/pallas_call | solution.py:354
  28.2 0.0 copy-start.7
  28.2 0.0 copy-done.1
  28.3 0.7 copy-done.7
  28.9 0.0 copy-start.2
  28.9 1.0 %copy-done.2 = bf16[4,8,16,512]{3,2,1,0:T(8,128)(2,1)S(1)} copy-done((bf16[4,8,16,512]{3,2,1,0:T(8,128)(2,1)S(1)}, bf16[4,8,16,512]{3,2,1,0:T(8,128)(2,1)}, u32[]{:S(2)}) %copy-start.2) | copy-done | bytes 524312
  30.0 0.0 copy-start.3
  30.0 1.0 %copy-done.3 = bf16[4,8,16,512]{3,2,1,0:T(8,128)(2,1)S(1)} copy-done((bf16[4,8,16,512]{3,2,1,0:T(8,128)(2,1)S(1)}, bf16[4,8,16,512]{3,2,1,0:T(8,128)(2,1)}, u32[]{:S(2)}) %copy-start.3) | copy-done | bytes 524312
  31.0 0.0 copy-start.5
  31.0 0.9 %copy-done.5 = bf16[2,4,2,4,16,128]{5,4,3,2,1,0:T(8,128)(2,1)S(1)} copy-done((bf16[2,4,2,4,16,128]{5,4,3,2,1,0:T(8,128)(2,1)S(1)}, bf16[2,4,2,4,16,128]{5,4,3,2,1,0:T(8,128)(2,1)}, u32[]{:S(2)}) %copy-start.5) | copy-done | bytes 262168
  32.0 0.0 copy-start.6
  32.0 0.8 %copy-done.6 = bf16[4,16,512]{2,1,0:T(8,128)(2,1)S(1)} copy-done((bf16[4,16,512]{2,1,0:T(8,128)(2,1)S(1)}, bf16[4,16,512]{2,1,0:T(8,128)(2,1)}, u32[]{:S(2)}) %copy-start.6) | copy-done | bytes 65560
  32.8 33.0 %conv.1 = (bf16[8,16,512]{2,1,0:T(8,128)(2,1)S(1)}, bf16[8,16,512]{2,1,0:T(8,128)(2,1)S(1)}, f32[27,16,64]{2,1,0:T(8,128)S(1)}) custom-call(s32[8,27]{1,0:T(8,128)S(1)} %copy-done.7, bf16[4,8,16,512]{3,2,1,0:T(8,128)(2,1)S(1)} %copy-done.2, bf16[4,8,16,512]{3,2,1,0:T(8,128)(2,1)S(1)} %copy-done.3, bf16[2,4,2,4,16,128]{5,4,3,2,1,0:T(8,128)(2,1)S(1)} %copy-done.5, ...), custom_call_target="tpu_custom_call" | custom-call | tf_op jit(solution)/shard_map/conv/pallas_call | solution.py:374
  65.8 0.7 copy.12
  66.4 0.7 copy.13
  67.1 0.7 %copy.14 = f32[27,16,64]{2,1,0:T(8,128)} copy(f32[27,16,64]{2,1,0:T(8,128)S(1)} %get-tuple-element.28) | data formatting | bytes 221184
  (2 shorter events, 0.0 us)
Async XLA Ops:
  0.6 1.0 %copy-start = (bf16[8,16,512]{2,1,0:T(8,128)(2,1)S(1)}, bf16[8,16,512]{2,1,0:T(8,128)(2,1)}, u32[]{:S(2)}) copy-start(bf16[8,16,512]{2,1,0:T(8,128)(2,1)} %cot.3) | copy-start | bytes 393220
  1.8 0.9 %copy-start.4 = (bf16[27,16,64]{2,1,0:T(8,128)(2,1)S(1)}, bf16[27,16,64]{2,1,0:T(8,128)(2,1)}, u32[]{:S(2)}) copy-start(bf16[27,16,64]{2,1,0:T(8,128)(2,1)} %weight.1) | copy-start | bytes 165892
  3.8 24.4 %copy-start.1 = (bf16[8,16,512]{2,1,0:T(8,128)(2,1)S(1)}, bf16[8,16,512]{2,1,0:T(8,128)(2,1)}, u32[]{:S(2)}) copy-start(bf16[8,16,512]{2,1,0:T(8,128)(2,1)} %cot.3) | copy-start | bytes 393220
  28.2 0.7 %copy-start.7 = (s32[8,27]{1,0:T(8,128)S(1)}, s32[8,27]{1,0:T(8,128)}, u32[]{:S(2)}) copy-start(s32[8,27]{1,0:T(8,128)} %table.1) | copy-start | bytes 2596
  28.9 1.0 %copy-start.2 = (bf16[4,8,16,512]{3,2,1,0:T(8,128)(2,1)S(1)}, bf16[4,8,16,512]{3,2,1,0:T(8,128)(2,1)}, u32[]{:S(2)}) copy-start(bf16[4,8,16,512]{3,2,1,0:T(8,128)(2,1)} %get-tuple-element.7.all_feat) | copy-start | bytes 1572868
  30.0 1.0 %copy-start.3 = (bf16[4,8,16,512]{3,2,1,0:T(8,128)(2,1)S(1)}, bf16[4,8,16,512]{3,2,1,0:T(8,128)(2,1)}, u32[]{:S(2)}) copy-start(bf16[4,8,16,512]{3,2,1,0:T(8,128)(2,1)} %get-tuple-element.8.all_cot) | copy-start | bytes 1572868
  31.0 0.9 %copy-start.5 = (bf16[2,4,2,4,16,128]{5,4,3,2,1,0:T(8,128)(2,1)S(1)}, bf16[2,4,2,4,16,128]{5,4,3,2,1,0:T(8,128)(2,1)}, u32[]{:S(2)}) copy-start(bf16[2,4,2,4,16,128]{5,4,3,2,1,0:T(8,128)(2,1)} %get-tuple-element.9.all_planes) | copy-start | bytes 786436
  32.0 0.8 %copy-start.6 = (bf16[4,16,512]{2,1,0:T(8,128)(2,1)S(1)}, bf16[4,16,512]{2,1,0:T(8,128)(2,1)}, u32[]{:S(2)}) copy-start(bf16[4,16,512]{2,1,0:T(8,128)(2,1)} %get-tuple-element.10.all_wcut) | copy-start | bytes 196612

commit v3 on v2

--- a/solution.py
+++ b/solution.py
@@ -27,7 +27,8 @@
 
 def gather_kernel(
     n_space, feat, cot, planes, wcut, all_feat, all_cot, all_planes, all_wcut,
-    local_sem, ring_send, ring_recv, fwd_send, fwd_recv, plane_send, plane_recv, w_send, w_recv,
+    ring_send, ring_recv, fwd_send, fwd_recv, face_send, face_recv,
+    side_send, side_recv, last_send, last_recv, w_send, w_recv,
 ):
     me = lax.axis_index("chan")
     here = lax.axis_index("space")
@@ -38,97 +39,91 @@
     for other in (right, left, across):
         pl.semaphore_signal(barrier, inc=1, device_id=(here, other), device_id_type=MESH)
     for place in (after, before):
-        for turn in range(4):
-            pl.semaphore_signal(
-                barrier, inc=1, device_id=(place, lax.rem(me + turn, 4)), device_id_type=MESH
-            )
-    pl.semaphore_wait(barrier, 11)
-
+        pl.semaphore_signal(barrier, inc=1, device_id=(place, me), device_id_type=MESH)
+    pl.semaphore_wait(barrier, 5)
+
+    peers = (right, left)
+    sources = (left, right)
     pairs = ((feat, all_feat), (cot, all_cot))
-    firsts = []
-    for order in range(2):
-        for tensor, (own, every) in enumerate(pairs):
-            for side, peer in enumerate((right, left)):
-                half = order if side == 0 else 1 - order
-                rows = pl.ds(HALF * half, HALF)
-                copy = push(
-                    own.at[rows], every.at[me, rows],
-                    ring_send.at[side, half, tensor], ring_recv.at[side, half, tensor], (here, peer),
-                )
-                copy.start()
-                firsts.append(copy)
-    others = []
-    for direction, place in enumerate((after, before)):
-        for turn in range(4):
-            copy = push(
-                planes.at[direction], all_planes.at[direction, me],
-                plane_send.at[direction, turn], plane_recv.at[direction, turn],
-                (place, lax.rem(me + turn, 4)),
-            )
-            copy.start()
-            others.append((copy, direction, turn))
-    weights = []
+
+    def face(direction):
+        return push(
+            planes.at[direction], all_planes.at[direction, me],
+            face_send.at[direction], face_recv.at[direction], ((after, before)[direction], me),
+        )
+
+    def ring(side, half, tensor, owner):
+        own, every = pairs[tensor]
+        rows = pl.ds(HALF * half, HALF)
+        return push(
+            own.at[rows], every.at[owner, rows],
+            ring_send.at[side, half, tensor], ring_recv.at[side, half, tensor], (here, peers[side]),
+        )
+
+    def relay(side, tensor, owner):
+        every = pairs[tensor][1]
+        rows = pl.ds(HALF * side, HALF)
+        return push(
+            every.at[owner, rows], every.at[owner, rows],
+            fwd_send.at[side, tensor], fwd_recv.at[side, tensor], (here, peers[side]),
+        )
+
+    def beside(side, direction, owner):
+        return push(
+            all_planes.at[direction, owner], all_planes.at[direction, owner],
+            side_send.at[side, direction], side_recv.at[side, direction], (here, peers[side]),
+        )
+
+    def onward(side, owner):
+        return push(
+            all_planes.at[side, owner], all_planes.at[side, owner],
+            last_send.at[side], last_recv.at[side], (here, peers[side]),
+        )
+
+    def columns(turn, owner, peer):
+        return push(
+            wcut.at[peer], all_wcut.at[owner], w_send.at[turn - 1], w_recv.at[turn - 1], (here, peer)
+        )
+
+    sent = []
+
+    def go(copy):
+        copy.start()
+        sent.append(copy)
+
+    for direction in range(2):
+        go(face(direction))
+    for tensor in range(2):
+        for side in range(2):
+            go(ring(side, side, tensor, me))
+    for direction in range(2):
+        face(direction).wait_recv()
+    for direction in range(2):
+        for side in range(2):
+            go(beside(side, side ^ direction, me))
     for turn in range(1, 4):
-        peer = lax.rem(me + turn, 4)
-        copy = push(
-            wcut.at[peer], all_wcut.at[me], w_send.at[turn - 1], w_recv.at[turn - 1], (here, peer)
-        )
-        copy.start()
-        weights.append((copy, turn))
-    locals_ = [
-        pltpu.make_async_copy(feat, all_feat.at[me], local_sem.at[0]),
-        pltpu.make_async_copy(cot, all_cot.at[me], local_sem.at[1]),
-        pltpu.make_async_copy(wcut.at[me], all_wcut.at[me], local_sem.at[2]),
-    ]
-    for copy in locals_:
-        copy.start()
-
-    seconds = []
-    for tensor, (own, every) in enumerate(pairs):
-        for side, (source, peer) in enumerate(((left, right), (right, left))):
-            half = side
-            rows = pl.ds(HALF * half, HALF)
-            push(
-                own.at[rows], every.at[source, rows],
-                ring_send.at[side, half, tensor], ring_recv.at[side, half, tensor], (here, peer),
-            ).wait_recv()
-            copy = push(
-                every.at[source, rows], every.at[source, rows],
-                fwd_send.at[side, tensor], fwd_recv.at[side, tensor], (here, peer),
-            )
-            copy.start()
-            seconds.append(copy)
-    for tensor, (own, every) in enumerate(pairs):
-        for side, source in enumerate((left, right)):
-            half = 1 - side
-            rows = pl.ds(HALF * half, HALF)
-            push(
-                own.at[rows], every.at[source, rows],
-                ring_send.at[side, half, tensor], ring_recv.at[side, half, tensor], (here, source),
-            ).wait_recv()
-            rows = pl.ds(HALF * side, HALF)
-            push(
-                every.at[across, rows], every.at[across, rows],
-                fwd_send.at[side, tensor], fwd_recv.at[side, tensor], (here, source),
-            ).wait_recv()
-    for copy, direction, turn in others:
-        source = lax.rem(me + 4 - turn, 4)
-        push(
-            planes.at[direction], all_planes.at[direction, source],
-            plane_send.at[direction, turn], plane_recv.at[direction, turn], (before, source),
-        ).wait_recv()
-    for copy, turn in weights:
-        source = lax.rem(me + 4 - turn, 4)
-        push(
-            wcut.at[source], all_wcut.at[source], w_send.at[turn - 1], w_recv.at[turn - 1], (here, source)
-        ).wait_recv()
-    for copy in locals_:
-        copy.wait()
-    for copy in firsts + seconds:
-        copy.wait_send()
-    for copy, direction, turn in others:
-        copy.wait_send()
-    for copy, turn in weights:
+        go(columns(turn, me, lax.rem(me + turn, 4)))
+    for tensor in range(2):
+        for side in range(2):
+            go(ring(side, 1 - side, tensor, me))
+    for tensor in range(2):
+        for side in range(2):
+            ring(side, side, tensor, sources[side]).wait_recv()
+            go(relay(side, tensor, sources[side]))
+    for side in range(2):
+        beside(side, side, sources[side]).wait_recv()
+        go(onward(side, sources[side]))
+    for side in range(2):
+        beside(side, 1 - side, sources[side]).wait_recv()
+    for turn in range(1, 4):
+        origin = lax.rem(me + 4 - turn, 4)
+        columns(turn, origin, origin).wait_recv()
+    for side in range(2):
+        for tensor in range(2):
+            ring(side, 1 - side, tensor, sources[side]).wait_recv()
+            relay(side, tensor, across).wait_recv()
+        onward(side, across).wait_recv()
+    for copy in sent:
         copy.wait_send()
 
 
@@ -237,8 +232,8 @@
 
 
 def conv_kernel(
-    inner, outer, scale, table, all_feat, all_cot, all_planes, all_wcut, cot, weight,
-    out, grad_in, result,
+    inner, outer, scale, table_at, feat_at, cot_at, planes_at, wcut_at, own_feat, own_cot, own_wcut, cot, weight,
+    out, grad_in, result, table, all_feat, all_cot, all_planes, all_wcut, load_sem,
     bricks, prev, nxt, wt, stage, rows, acc, part, pieces, tile, blocks, whole,
     a_send, a_recv, b_send, b_recv, c_send, c_recv,
 ):
@@ -259,6 +254,27 @@
     for d in range(1, outer):
         peer = lax.rem(block + d, outer) * inner + rank
         pl.semaphore_signal(barrier, inc=1, device_id=(peer, chan), device_id_type=MESH)
+    loads = [
+        pltpu.make_async_copy(table_at, table, load_sem.at[0]),
+        pltpu.make_async_copy(planes_at, all_planes, load_sem.at[1]),
+        pltpu.make_async_copy(own_feat, all_feat.at[chan], load_sem.at[2]),
+        pltpu.make_async_copy(own_cot, all_cot.at[chan], load_sem.at[3]),
+        pltpu.make_async_copy(own_wcut.at[chan], all_wcut.at[chan], load_sem.at[4]),
+    ]
+    for turn in range(1, 4):
+        origin = lax.rem(chan + turn, 4)
+        for place, (source, target) in enumerate(
+            ((feat_at, all_feat), (cot_at, all_cot), (wcut_at, all_wcut))
+        ):
+            loads.append(
+                pltpu.make_async_copy(
+                    source.at[origin], target.at[origin], load_sem.at[2 + 3 * turn + place]
+                )
+            )
+    for copy in loads:
+        copy.start()
+    for copy in loads:
+        copy.wait()
     assemble_all(
         scale, table, all_feat, all_cot, all_planes, all_wcut, cot, weight,
         bricks, prev, nxt, wt, stage, rows, acc, part,
@@ -337,7 +353,6 @@
     outer = n_space // inner
     vmem = pl.BlockSpec(memory_space=pltpu.VMEM)
     anyspace = pl.BlockSpec(memory_space=pl.ANY)
-    smem = pl.BlockSpec(memory_space=pltpu.SMEM)
     bf16, f32 = jnp.bfloat16, jnp.float32
 
     sides = []
@@ -360,10 +375,10 @@
             jax.ShapeDtypeStruct((4, SHARE, 512), bf16),
         ),
         in_specs=[anyspace] * 4,
-        out_specs=(vmem,) * 4,
+        out_specs=(anyspace,) * 4,
         scratch_shapes=[
-            dma((3,)), dma((2, 2, 2)), dma((2, 2, 2)), dma((2, 2)), dma((2, 2)),
-            dma((2, 4)), dma((2, 4)), dma((3,)), dma((3,)),
+            dma((2, 2, 2)), dma((2, 2, 2)), dma((2, 2)), dma((2, 2)), dma((2,)), dma((2,)),
+            dma((2, 2)), dma((2, 2)), dma((2,)), dma((2,)), dma((3,)), dma((3,)),
         ],
         compiler_params=pltpu.CompilerParams(collective_id=0, has_side_effects=True),
         name="gather",
@@ -378,9 +393,15 @@
             jax.ShapeDtypeStruct((BRICKS, SHARE, 512), bf16),
             jax.ShapeDtypeStruct((27, SHARE, 64), f32),
         ),
-        in_specs=[smem] + [vmem] * 6,
+        in_specs=[pl.BlockSpec(memory_space=pltpu.HBM)] * 8 + [vmem] * 2,
         out_specs=(vmem,) * 3,
         scratch_shapes=[
+            pltpu.SMEM((BRICKS, 27), jnp.int32),
+            pltpu.VMEM((4, BRICKS, SHARE, 512), bf16),
+            pltpu.VMEM((4, BRICKS, SHARE, 512), bf16),
+            pltpu.VMEM((2, 4, 2, BRICKS // 2, SHARE, 128), bf16),
+            pltpu.VMEM((4, SHARE, 512), bf16),
+            dma((14,)),
             pltpu.VMEM((BRICKS + 1, 8, 8, 8, 128), f32),
             pltpu.VMEM((BRICKS + 1, 8, 8, 128), f32),
             pltpu.VMEM((BRICKS + 1, 8, 8, 128), f32),
@@ -397,10 +418,12 @@
             dma((inner,)), dma((inner,)),
         ],
         compiler_params=pltpu.CompilerParams(
-            collective_id=1, has_side_effects=True, vmem_limit_bytes=48 * 2**20
+            collective_id=1, has_side_effects=True, vmem_limit_bytes=63 * 2**20
         ),
         name="conv",
-    )(neighbours, all_feat, all_cot, all_planes, all_wcut, cotangent, weight)
+    )(
+        neighbours, all_feat, all_cot, all_planes, all_wcut, features, cotangent, wcut, cotangent, weight
+    )
     return (output, grad_input, grad_weight)
 
 

time: 68.1 us -> 64.5 us (0.947)
  local copies, waits for them, and re-layouts: 8.88 us -> 5.3 us
    unnamed x19 -> x11, local copies, waits for them, and re-layouts: 6.79 us -> 3.21 us
    pallas_call x1, Pallas kernels: 24.4 us -> 26.8 us  [body(): pl.pallas_call(functools.partial(gather_kernel, n_space), out_shape=(jax....]
    pallas_call x1, Pallas kernels: 33 us -> 30.6 us  [body(): pl.pallas_call(functools.partial(conv_kernel, inner, outer, voxels ** (-0...]
where the time goes in v3:
time: 64.5 us; the launch traced here: 64.3 us
  Pallas kernels  57.4 us (89%)
  local copies, waits for them, and re-layouts  5.3 us (8%)
  other arithmetic  0.82 us (1%)
  between operations  0.72 us (1%)
    pallas_call x1, Pallas kernels, body(): pl.pallas_call(functools.partial(conv_kernel, inner, outer, voxels ** (-0...  30.6 us
    pallas_call x1, Pallas kernels, body(): pl.pallas_call(functools.partial(gather_kernel, n_space), out_shape=(jax....  26.8 us
    unnamed x11, local copies, waits for them, and re-layouts  3.21 us

profile of v3, /device:TPU:1, one launch (start us, length us, event | category | flops | bytes accessed | tf_op | source)
XLA Modules:
  0.0 64.3 jit_solution(11087656896659114599)
XLA Ops:
  0.6 0.0 copy-start
  0.6 0.9 %fusion = (bf16[4,16,64]{2,1,0:T(8,128)(2,1)S(1)}, bf16[4,16,64]{2,1,0:T(8,128)(2,1)S(1)}, bf16[4,16,64]{2,1,0:T(8,128)(2,1)S(1)}, bf16[4,16,64]{2,1,0:T(8,128)(2,1)S(1)}) fusion(bf16[8,16,512]{2,1,0:T(8,128)(2,1)} %own_feat.1), kind=kLoop, calls=%fused_computation.7 | loop fusion | bytes 65536 | tf_op jit(solution)/shard_map/slice | solution.py:361
  1.5 0.1 maximum_bitcast_fusion.2
  1.6 0.0 copy-done
  1.6 0.1 fusion.1
  1.7 0.1 maximum_bitcast_fusion.3
  1.8 0.0 copy-start.1
  1.8 0.6 pad_maximum_fusion.planes
  2.5 0.2 copy-done.1
  2.7 0.2 reshape.9
  2.9 0.2 copy.8
  3.2 0.7 %pad.4.wcut.own_wcut = bf16[4,16,512]{2,1,0:T(8,128)(2,1)} pad(bf16[4,16,432]{2,1,0:T(8,128)(2,1)S(1)} %copy.8, bf16[]{:T(256)} %constant.2.clone.1), padding=0_0x0_0x0_80 | pad | bytes 120834 | tf_op jit(solution)/shard_map/jit(_pad)/pad | solution.py:366
  3.9 26.8 %gather.1 = (bf16[4,8,16,512]{3,2,1,0:T(8,128)(2,1)}, bf16[4,8,16,512]{3,2,1,0:T(8,128)(2,1)}, bf16[2,4,2,4,16,128]{5,4,3,2,1,0:T(8,128)(2,1)}, bf16[4,16,512]{2,1,0:T(8,128)(2,1)}) custom-call(bf16[8,16,512]{2,1,0:T(8,128)(2,1)} %own_feat.1, bf16[8,16,512]{2,1,0:T(8,128)(2,1)} %cot.3, bf16[2,2,4,16,128]{4,3,2,1,0:T(8,128)(2,1)} %pad_maximum_fusion.planes, ...), custom_call_target="tpu_custom_call" | custom-call | tf_op jit(solution)/shard_map/gather/pallas_call | solution.py:369
  30.7 30.6 %conv.1 = (bf16[8,16,512]{2,1,0:T(8,128)(2,1)}, bf16[8,16,512]{2,1,0:T(8,128)(2,1)}, f32[27,16,64]{2,1,0:T(8,128)}) custom-call(s32[8,27]{1,0:T(8,128)} %table_at.1, bf16[4,8,16,512]{3,2,1,0:T(8,128)(2,1)} %get-tuple-element.7.feat_at, bf16[4,8,16,512]{3,2,1,0:T(8,128)(2,1)} %get-tuple-element.8.cot_at, ...), custom_call_target="tpu_custom_call" | custom-call | tf_op jit(solution)/shard_map/conv/pallas_call | solution.py:389
  61.3 0.0 copy-start.3
  61.3 0.0 copy-start.2
  61.3 1.6 %copy.12 = bf16[8,16,512]{2,1,0:T(8,128)(2,1)} copy(bf16[8,16,512]{2,1,0:T(8,128)(2,1)} %get-tuple-element.26) | data formatting | bytes 262144
  62.9 0.0 copy-done.3
  62.9 0.7 %copy.13 = bf16[8,16,512]{2,1,0:T(8,128)(2,1)} copy(bf16[8,16,512]{2,1,0:T(8,128)(2,1)S(1)} %copy-done.3) | data formatting | bytes 262144
  63.6 0.0 copy-done.2
  63.6 0.7 %copy.14 = f32[27,16,64]{2,1,0:T(8,128)} copy(f32[27,16,64]{2,1,0:T(8,128)S(1)} %copy-done.2) | data formatting | bytes 221184
  (2 shorter events, 0.0 us)
Async XLA Ops:
  0.6 1.0 %copy-start = (bf16[8,16,512]{2,1,0:T(8,128)(2,1)S(1)}, bf16[8,16,512]{2,1,0:T(8,128)(2,1)}, u32[]{:S(2)}) copy-start(bf16[8,16,512]{2,1,0:T(8,128)(2,1)} %cot.3) | copy-start | bytes 393220
  1.8 0.9 %copy-start.1 = (bf16[27,16,64]{2,1,0:T(8,128)(2,1)S(1)}, bf16[27,16,64]{2,1,0:T(8,128)(2,1)}, u32[]{:S(2)}) copy-start(bf16[27,16,64]{2,1,0:T(8,128)(2,1)} %weight.1) | copy-start | bytes 165892
  61.3 1.6 %copy-start.3 = (bf16[8,16,512]{2,1,0:T(8,128)(2,1)S(1)}, bf16[8,16,512]{2,1,0:T(8,128)(2,1)}, u32[]{:S(2)}) copy-start(bf16[8,16,512]{2,1,0:T(8,128)(2,1)} %get-tuple-element.27) | copy-start | bytes 393220
  61.3 2.3 %copy-start.2 = (f32[27,16,64]{2,1,0:T(8,128)S(1)}, f32[27,16,64]{2,1,0:T(8,128)}, u32[]{:S(2)}) copy-start(f32[27,16,64]{2,1,0:T(8,128)} %get-tuple-element.28) | copy-start | bytes 331780

commit v4 on v3

--- a/solution.py
+++ b/solution.py
@@ -25,8 +25,29 @@
     )
 
 
+def pack(feat, cot, weight, planes, wcut):
+    lane = lax.broadcasted_iota(jnp.int32, (SHARE, 128), 1)
+    for t, tensor in enumerate((feat, cot)):
+        for pair in range(BRICKS // 2):
+            for direction, lanes in enumerate((slice(384, 512), slice(0, 128))):
+                first = tensor[2 * pair, :, lanes].astype(jnp.float32)
+                second = tensor[2 * pair + 1, :, lanes].astype(jnp.float32)
+                if direction == 0:
+                    first = pltpu.roll(first, 64, 1)
+                else:
+                    second = pltpu.roll(second, 64, 1)
+                planes[direction, t, pair] = jnp.where(lane < 64, first, second).astype(jnp.bfloat16)
+    for g in range(4):
+        count = min(8, 27 - 8 * g)
+        block = weight[8 * g : 8 * g + count].reshape(SHARE * count, 64).astype(jnp.float32)
+        if count < 8:
+            block = jnp.concatenate([block, jnp.zeros((128 - SHARE * count, 64), jnp.float32)], axis=0)
+        wcut[:, :, 128 * g : 128 * g + 128] = block.T.reshape(4, SHARE, 128).astype(jnp.bfloat16)
+
+
 def gather_kernel(
-    n_space, feat, cot, planes, wcut, all_feat, all_cot, all_planes, all_wcut,
+    n_space, feat, cot, weight, all_feat, all_cot, all_planes, all_wcut,
+    feat_here, cot_here, weight_here, planes, wcut, local_sem,
     ring_send, ring_recv, fwd_send, fwd_recv, face_send, face_recv,
     side_send, side_recv, last_send, last_recv, w_send, w_recv,
 ):
@@ -35,11 +56,24 @@
     right, left, across = lax.rem(me + 1, 4), lax.rem(me + 3, 4), lax.rem(me + 2, 4)
     after, before = lax.rem(here + 1, n_space), lax.rem(here + n_space - 1, n_space)
 
+    loads = [
+        pltpu.make_async_copy(source, target, local_sem.at[place])
+        for place, (source, target) in enumerate(
+            ((feat, feat_here), (cot, cot_here), (weight, weight_here))
+        )
+    ]
+    for copy in loads:
+        copy.start()
     barrier = pltpu.get_barrier_semaphore()
     for other in (right, left, across):
         pl.semaphore_signal(barrier, inc=1, device_id=(here, other), device_id_type=MESH)
     for place in (after, before):
         pl.semaphore_signal(barrier, inc=1, device_id=(place, me), device_id_type=MESH)
+    for copy in loads:
+        copy.wait()
+    pack(feat_here, cot_here, weight_here, planes, wcut)
+    kept = pltpu.make_async_copy(wcut.at[me], all_wcut.at[me], local_sem.at[3])
+    kept.start()
     pl.semaphore_wait(barrier, 5)
 
     peers = (right, left)
@@ -123,33 +157,19 @@
             ring(side, 1 - side, tensor, sources[side]).wait_recv()
             relay(side, tensor, across).wait_recv()
         onward(side, across).wait_recv()
+    kept.wait()
     for copy in sent:
         copy.wait_send()
 
 
 def assemble_all(
-    scale, table, all_feat, all_cot, all_planes, all_wcut, cot, weight, bricks, prev, nxt, wt, stage, rows, acc, part
+    scale, table, all_feat, all_cot, all_planes, cot, bricks, prev, nxt, stage, rows, acc, part
 ):
     zero = jnp.zeros((8, 8, 128), jnp.float32)
     for u in range(8):
         bricks[BRICKS, u] = zero
     prev[BRICKS] = zero
     nxt[BRICKS] = zero
-    wt[...] = jnp.zeros((128, 1152), jnp.bfloat16)
-    lane = lax.broadcasted_iota(jnp.int32, (SHARE, 128), 1)
-    for a in range(3):
-        for j in range(9):
-            k = 9 * a + j
-            wt[32 * a : 32 * a + 16, 128 * j : 128 * j + 64] = weight[k]
-            back = 26 - k
-            block = jnp.zeros((SHARE, 128), jnp.float32)
-            for p in range(4):
-                start = 64 + SHARE * p
-                piece = all_wcut[p, :, 128 * (back // 8) : 128 * (back // 8) + 128].astype(jnp.float32)
-                piece = pltpu.roll(piece, (start - SHARE * (back % 8)) % 128, 1)
-                block = jnp.where((lane >= start) & (lane < start + SHARE), piece, block)
-            wt[32 * a + 16 : 32 * a + 32, 128 * j : 128 * j + 128] = block.astype(jnp.bfloat16)
-
     def turn_brick(s, carry):
         both = jnp.concatenate(
             [all_feat[:, s].reshape(64, 512), all_cot[:, s].reshape(64, 512)], axis=0
@@ -213,6 +233,23 @@
         part[k] = jnp.zeros((8, 128), jnp.float32)
 
 
+def lay_weights(weight, all_wcut, wt):
+    wt[...] = jnp.zeros((128, 1152), jnp.bfloat16)
+    lane = lax.broadcasted_iota(jnp.int32, (SHARE, 128), 1)
+    for a in range(3):
+        for j in range(9):
+            k = 9 * a + j
+            wt[32 * a : 32 * a + 16, 128 * j : 128 * j + 64] = weight[k]
+            back = 26 - k
+            block = jnp.zeros((SHARE, 128), jnp.float32)
+            for p in range(4):
+                start = 64 + SHARE * p
+                piece = all_wcut[p, :, 128 * (back // 8) : 128 * (back // 8) + 128].astype(jnp.float32)
+                piece = pltpu.roll(piece, (start - SHARE * (back % 8)) % 128, 1)
+                block = jnp.where((lane >= start) & (lane < start + SHARE), piece, block)
+            wt[32 * a + 16 : 32 * a + 32, 128 * j : 128 * j + 128] = block.astype(jnp.bfloat16)
+
+
 def convolve(first, last, rows, wt, out, grad_in):
     def one_brick(r, carry):
         terms = lax.dot_general(
@@ -232,7 +269,7 @@
 
 
 def conv_kernel(
-    inner, outer, scale, table_at, feat_at, cot_at, planes_at, wcut_at, own_feat, own_cot, own_wcut, cot, weight,
+    inner, outer, scale, table_at, feat_at, cot_at, planes_at, wcut_at, own_feat, own_cot, cot, weight,
     out, grad_in, result, table, all_feat, all_cot, all_planes, all_wcut, load_sem,
     bricks, prev, nxt, wt, stage, rows, acc, part, pieces, tile, blocks, whole,
     a_send, a_recv, b_send, b_recv, c_send, c_recv,
@@ -259,16 +296,16 @@
         pltpu.make_async_copy(planes_at, all_planes, load_sem.at[1]),
         pltpu.make_async_copy(own_feat, all_feat.at[chan], load_sem.at[2]),
         pltpu.make_async_copy(own_cot, all_cot.at[chan], load_sem.at[3]),
-        pltpu.make_async_copy(own_wcut.at[chan], all_wcut.at[chan], load_sem.at[4]),
+        pltpu.make_async_copy(wcut_at, all_wcut, load_sem.at[4]),
     ]
     for turn in range(1, 4):
         origin = lax.rem(chan + turn, 4)
         for place, (source, target) in enumerate(
-            ((feat_at, all_feat), (cot_at, all_cot), (wcut_at, all_wcut))
+            ((feat_at, all_feat), (cot_at, all_cot))
         ):
             loads.append(
                 pltpu.make_async_copy(
-                    source.at[origin], target.at[origin], load_sem.at[2 + 3 * turn + place]
+                    source.at[origin], target.at[origin], load_sem.at[3 + 2 * turn + place]
                 )
             )
     for copy in loads:
@@ -276,8 +313,7 @@
     for copy in loads:
         copy.wait()
     assemble_all(
-        scale, table, all_feat, all_cot, all_planes, all_wcut, cot, weight,
-        bricks, prev, nxt, wt, stage, rows, acc, part,
+        scale, table, all_feat, all_cot, all_planes, cot, bricks, prev, nxt, stage, rows, acc, part
     )
     pl.semaphore_wait(barrier, inner - 1 + outer - 1)
 
@@ -298,6 +334,7 @@
 
     lax.fori_loop(1, inner, start_scatter, 0)
     pieces[0] = part[pl.ds(rank * share, share)]
+    lay_weights(weight, all_wcut, wt)
     convolve(0, BRICKS // 2, rows, wt, out, grad_in)
     lax.fori_loop(1, inner, wait_scatter, 0)
     tile[...] = jnp.sum(pieces[...], axis=0)
@@ -354,16 +391,6 @@
     vmem = pl.BlockSpec(memory_space=pltpu.VMEM)
     anyspace = pl.BlockSpec(memory_space=pl.ANY)
     bf16, f32 = jnp.bfloat16, jnp.float32
-
-    sides = []
-    for lanes in (slice(448, 512), slice(0, 64)):
-        both = [
-            jnp.concatenate([t[0::2, :, lanes], t[1::2, :, lanes]], axis=2) for t in (features, cotangent)
-        ]
-        sides.append(jnp.stack(both))
-    planes = jnp.stack(sides)
-    wcut = weight.transpose(2, 0, 1).reshape(4, SHARE, 27 * SHARE)
-    wcut = jnp.pad(wcut, ((0, 0), (0, 0), (0, 512 - 27 * SHARE)))
 
     dma = pltpu.SemaphoreType.DMA
     all_feat, all_cot, all_planes, all_wcut = pl.pallas_call(
@@ -374,15 +401,21 @@
             jax.ShapeDtypeStruct((2, 4, 2, BRICKS // 2, SHARE, 128), bf16),
             jax.ShapeDtypeStruct((4, SHARE, 512), bf16),
         ),
-        in_specs=[anyspace] * 4,
+        in_specs=[anyspace] * 3,
         out_specs=(anyspace,) * 4,
         scratch_shapes=[
+            pltpu.VMEM((BRICKS, SHARE, 512), bf16),
+            pltpu.VMEM((BRICKS, SHARE, 512), bf16),
+            pltpu.VMEM((27, SHARE, 64), bf16),
+            pltpu.VMEM((2, 2, BRICKS // 2, SHARE, 128), bf16),
+            pltpu.VMEM((4, SHARE, 512), bf16),
+            dma((4,)),
             dma((2, 2, 2)), dma((2, 2, 2)), dma((2, 2)), dma((2, 2)), dma((2,)), dma((2,)),
             dma((2, 2)), dma((2, 2)), dma((2,)), dma((2,)), dma((3,)), dma((3,)),
         ],
         compiler_params=pltpu.CompilerParams(collective_id=0, has_side_effects=True),
         name="gather",
-    )(features, cotangent, planes, wcut)
+    )(features, cotangent, weight)
 
     voxels = n_space * BRICKS * 512
     share = KERNEL_TILES // inner
@@ -393,7 +426,7 @@
             jax.ShapeDtypeStruct((BRICKS, SHARE, 512), bf16),
             jax.ShapeDtypeStruct((27, SHARE, 64), f32),
         ),
-        in_specs=[pl.BlockSpec(memory_space=pltpu.HBM)] * 8 + [vmem] * 2,
+        in_specs=[pl.BlockSpec(memory_space=pltpu.HBM)] * 7 + [vmem] * 2,
         out_specs=(vmem,) * 3,
         scratch_shapes=[
             pltpu.SMEM((BRICKS, 27), jnp.int32),
@@ -401,7 +434,7 @@
             pltpu.VMEM((4, BRICKS, SHARE, 512), bf16),
             pltpu.VMEM((2, 4, 2, BRICKS // 2, SHARE, 128), bf16),
             pltpu.VMEM((4, SHARE, 512), bf16),
-            dma((14,)),
+            dma((11,)),
             pltpu.VMEM((BRICKS + 1, 8, 8, 8, 128), f32),
             pltpu.VMEM((BRICKS + 1, 8, 8, 128), f32),
             pltpu.VMEM((BRICKS + 1, 8, 8, 128), f32),
@@ -422,7 +455,7 @@
         ),
         name="conv",
     )(
-        neighbours, all_feat, all_cot, all_planes, all_wcut, features, cotangent, wcut, cotangent, weight
+        neighbours, all_feat, all_cot, all_planes, all_wcut, features, cotangent, cotangent, weight
     )
     return (output, grad_input, grad_weight)
 

time: 64.5 us -> 61.1 us (0.947)
  local copies, waits for them, and re-layouts: 5.3 us -> 2.96 us
  other arithmetic: 0.82 us -> 0 us
    slice x2 -> x0, local copies, waits for them, and re-layouts: 0.97 us -> none  [body(): t[0::2, :, lanes]]
    another operation x5 -> x0, other arithmetic: 0.82 us -> none  [the longest x3 0.65 us: body(): planes = jnp.stack(sides)]
    pad x1 -> x0, local copies, waits for them, and re-layouts: 0.66 us -> none  [body(): wcut = jnp.pad(wcut, ((0, 0), (0, 0), (0, 512 - 27 * SHARE)))]
    unnamed x11 -> x7, local copies, waits for them, and re-layouts: 3.21 us -> 2.96 us
where the time goes in v4:
time: 61.1 us; the launch traced here: 60.9 us
  Pallas kernels  57.3 us (94%)
  local copies, waits for them, and re-layouts  2.96 us (5%)
  between operations  0.66 us (1%)
    pallas_call x1, Pallas kernels, body(): pl.pallas_call(functools.partial(conv_kernel, inner, outer, voxels ** (-0...  30.4 us
    pallas_call x1, Pallas kernels, body(): pl.pallas_call(functools.partial(gather_kernel, n_space), out_shape=(jax....  26.9 us
    unnamed x7, local copies, waits for them, and re-layouts  2.96 us

profile of v4, /device:TPU:1, one launch (start us, length us, event | category | flops | bytes accessed | tf_op | source)
XLA Modules:
  0.0 60.9 jit_solution(1938205449331515018)
XLA Ops:
  0.6 26.9 %gather.1 = (bf16[4,8,16,512]{3,2,1,0:T(8,128)(2,1)}, bf16[4,8,16,512]{3,2,1,0:T(8,128)(2,1)}, bf16[2,4,2,4,16,128]{5,4,3,2,1,0:T(8,128)(2,1)}, bf16[4,16,512]{2,1,0:T(8,128)(2,1)}) custom-call(bf16[8,16,512]{2,1,0:T(8,128)(2,1)} %own_feat.1, bf16[8,16,512]{2,1,0:T(8,128)(2,1)} %cot.3, bf16[27,16,64]{2,1,0:T(8,128)(2,1)} %weight.3), custom_call_target="tpu_custom_call" | custom-call | tf_op jit(solution)/shard_map/gather/pallas_call | solution.py:396
  27.5 30.4 %conv.1 = (bf16[8,16,512]{2,1,0:T(8,128)(2,1)}, bf16[8,16,512]{2,1,0:T(8,128)(2,1)}, f32[27,16,64]{2,1,0:T(8,128)}) custom-call(s32[8,27]{1,0:T(8,128)} %table_at.1, bf16[4,8,16,512]{3,2,1,0:T(8,128)(2,1)} %get-tuple-element.7.feat_at, bf16[4,8,16,512]{3,2,1,0:T(8,128)(2,1)} %get-tuple-element.8.cot_at, ...), custom_call_target="tpu_custom_call" | custom-call | tf_op jit(solution)/shard_map/conv/pallas_call | solution.py:422
  57.9 0.0 copy-start.1
  57.9 0.0 copy-start
  57.9 1.6 %copy.10 = bf16[8,16,512]{2,1,0:T(8,128)(2,1)} copy(bf16[8,16,512]{2,1,0:T(8,128)(2,1)} %get-tuple-element.14) | data formatting | bytes 262144
  59.5 0.0 copy-done.1
  59.5 0.7 %copy.11 = bf16[8,16,512]{2,1,0:T(8,128)(2,1)} copy(bf16[8,16,512]{2,1,0:T(8,128)(2,1)S(1)} %copy-done.1) | data formatting | bytes 262144
  60.2 0.0 copy-done
  60.2 0.7 %copy.12 = f32[27,16,64]{2,1,0:T(8,128)} copy(f32[27,16,64]{2,1,0:T(8,128)S(1)} %copy-done) | data formatting | bytes 221184
Async XLA Ops:
  57.9 1.6 %copy-start.1 = (bf16[8,16,512]{2,1,0:T(8,128)(2,1)S(1)}, bf16[8,16,512]{2,1,0:T(8,128)(2,1)}, u32[]{:S(2)}) copy-start(bf16[8,16,512]{2,1,0:T(8,128)(2,1)} %get-tuple-element.15) | copy-start | bytes 393220
  57.9 2.3 %copy-start = (f32[27,16,64]{2,1,0:T(8,128)S(1)}, f32[27,16,64]{2,1,0:T(8,128)}, u32[]{:S(2)}) copy-start(f32[27,16,64]{2,1,0:T(8,128)} %get-tuple-element.16) | copy-start | bytes 331780

commit v5 on v4

--- a/solution.py
+++ b/solution.py
@@ -177,7 +177,7 @@
         bricks[s] = both.astype(jnp.float32).T.reshape(8, 8, 8, 128)
         return carry
 
-    lax.fori_loop(0, BRICKS, turn_brick, 0)
+    lax.fori_loop(0, BRICKS, turn_brick, 0, unroll=True)
     for direction, held in enumerate((prev, nxt)):
         for pair in range(BRICKS // 2):
             both = jnp.concatenate(
@@ -187,7 +187,7 @@
 
     acc[...] = jnp.zeros(acc.shape, jnp.float32)
 
-    def one_brick(r, carry):
+    def one_brick(r, side):
         def slot(i, j, k):
             named = table[r, 9 * i + 3 * j + k]
             return jnp.where(named < 0, BRICKS, jnp.bitwise_and(named, BRICKS - 1))
@@ -204,15 +204,15 @@
                     else:
                         low, mid, high = [(prev, None, nxt)[i][s, vs] for s in ids]
                     w = lax.broadcasted_iota(jnp.int32, mid.shape, 1)
-                    stage[0, x, ys] = pltpu.roll(jnp.where(w == 7, low, mid), 1, 1)
-                    stage[1, x, ys] = mid
-                    stage[2, x, ys] = pltpu.roll(jnp.where(w == 0, high, mid), 7, 1)
+                    stage[side, 0, x, ys] = pltpu.roll(jnp.where(w == 7, low, mid), 1, 1)
+                    stage[side, 1, x, ys] = mid
+                    stage[side, 2, x, ys] = pltpu.roll(jnp.where(w == 0, high, mid), 7, 1)
         for b in range(3):
             for c in range(3):
                 j = 3 * b + c
                 for x in range(10):
                     rows[r, 64 * x : 64 * x + 64, 128 * j : 128 * j + 128] = (
-                        stage[c, x, b : b + 8].reshape(64, 128).astype(jnp.bfloat16)
+                        stage[side, c, x, b : b + 8].reshape(64, 128).astype(jnp.bfloat16)
                     )
         wide = jnp.concatenate(
             [cot[r].astype(jnp.float32), jnp.zeros((SHARE, 128), jnp.float32)], axis=1
@@ -221,9 +221,13 @@
         acc[...] += jnp.dot(
             lifted.astype(jnp.bfloat16), rows[r], preferred_element_type=jnp.float32
         )
-        return carry
-
-    lax.fori_loop(0, BRICKS, one_brick, 0)
+
+    def two_bricks(t, carry):
+        one_brick(2 * t, 0)
+        one_brick(2 * t + 1, 1)
+        return carry
+
+    lax.fori_loop(0, BRICKS // 2, two_bricks, 0)
     lane = lax.broadcasted_iota(jnp.int32, (8, 128), 1)
     for a in range(3):
         for j in range(9):
@@ -265,7 +269,7 @@
         grad_in[r] = total[16:32].astype(jnp.bfloat16)
         return carry
 
-    lax.fori_loop(first, last, one_brick, 0)
+    lax.fori_loop(first, last, one_brick, 0, unroll=True)
 
 
 def conv_kernel(
@@ -439,7 +443,7 @@
             pltpu.VMEM((BRICKS + 1, 8, 8, 128), f32),
             pltpu.VMEM((BRICKS + 1, 8, 8, 128), f32),
             pltpu.VMEM((128, 1152), bf16),
-            pltpu.VMEM((3, 10, 10, 8, 128), f32),
+            pltpu.VMEM((2, 3, 10, 10, 8, 128), f32),
             pltpu.VMEM((BRICKS, 640, 1152), bf16),
             pltpu.VMEM((48, 1152), f32),
             pltpu.VMEM((KERNEL_TILES, 8, 128), f32),

time: 61.1 us -> 59.5 us (0.974)
  Pallas kernels: 57.3 us -> 55.7 us
    pallas_call x1, Pallas kernels: 30.4 us -> 28.8 us  [body(): pl.pallas_call(functools.partial(conv_kernel, inner, outer, voxels ** (-0...]
where the time goes in v5:
time: 59.5 us; the launch traced here: 59.3 us
  Pallas kernels  55.7 us (94%)
  local copies, waits for them, and re-layouts  2.96 us (5%)
  between operations  0.66 us (1%)
    pallas_call x1, Pallas kernels, body(): pl.pallas_call(functools.partial(conv_kernel, inner, outer, voxels ** (-0...  28.8 us
    pallas_call x1, Pallas kernels, body(): pl.pallas_call(functools.partial(gather_kernel, n_space), out_shape=(jax....  26.9 us
    unnamed x7, local copies, waits for them, and re-layouts  2.96 us

profile of v5, /device:TPU:1, one launch (start us, length us, event | category | flops | bytes accessed | tf_op | source)
XLA Modules:
  0.0 59.3 jit_solution(18054161806039615858)
XLA Ops:
  0.6 26.9 %gather.1 = (bf16[4,8,16,512]{3,2,1,0:T(8,128)(2,1)}, bf16[4,8,16,512]{3,2,1,0:T(8,128)(2,1)}, bf16[2,4,2,4,16,128]{5,4,3,2,1,0:T(8,128)(2,1)}, bf16[4,16,512]{2,1,0:T(8,128)(2,1)}) custom-call(bf16[8,16,512]{2,1,0:T(8,128)(2,1)} %own_feat.1, bf16[8,16,512]{2,1,0:T(8,128)(2,1)} %cot.3, bf16[27,16,64]{2,1,0:T(8,128)(2,1)} %weight.3), custom_call_target="tpu_custom_call" | custom-call | tf_op jit(solution)/shard_map/gather/pallas_call | solution.py:400
  27.5 28.8 %conv.1 = (bf16[8,16,512]{2,1,0:T(8,128)(2,1)}, bf16[8,16,512]{2,1,0:T(8,128)(2,1)}, f32[27,16,64]{2,1,0:T(8,128)}) custom-call(s32[8,27]{1,0:T(8,128)} %table_at.1, bf16[4,8,16,512]{3,2,1,0:T(8,128)(2,1)} %get-tuple-element.7.feat_at, bf16[4,8,16,512]{3,2,1,0:T(8,128)(2,1)} %get-tuple-element.8.cot_at, ...), custom_call_target="tpu_custom_call" | custom-call | tf_op jit(solution)/shard_map/conv/pallas_call | solution.py:426
  56.3 0.0 copy-start.1
  56.3 0.0 copy-start
  56.4 1.6 %copy.10 = bf16[8,16,512]{2,1,0:T(8,128)(2,1)} copy(bf16[8,16,512]{2,1,0:T(8,128)(2,1)} %get-tuple-element.14) | data formatting | bytes 262144
  58.0 0.0 copy-done.1
  58.0 0.7 %copy.11 = bf16[8,16,512]{2,1,0:T(8,128)(2,1)} copy(bf16[8,16,512]{2,1,0:T(8,128)(2,1)S(1)} %copy-done.1) | data formatting | bytes 262144
  58.6 0.0 copy-done
  58.6 0.7 %copy.12 = f32[27,16,64]{2,1,0:T(8,128)} copy(f32[27,16,64]{2,1,0:T(8,128)S(1)} %copy-done) | data formatting | bytes 221184
Async XLA Ops:
  56.3 1.6 %copy-start.1 = (bf16[8,16,512]{2,1,0:T(8,128)(2,1)S(1)}, bf16[8,16,512]{2,1,0:T(8,128)(2,1)}, u32[]{:S(2)}) copy-start(bf16[8,16,512]{2,1,0:T(8,128)(2,1)} %get-tuple-element.15) | copy-start | bytes 393220
  56.3 2.3 %copy-start = (f32[27,16,64]{2,1,0:T(8,128)S(1)}, f32[27,16,64]{2,1,0:T(8,128)}, u32[]{:S(2)}) copy-start(f32[27,16,64]{2,1,0:T(8,128)} %get-tuple-element.16) | copy-start | bytes 331780
